TPU v7x, 256 devices: a whole 4x4x8 slice. The times are simulated.
256 devices in a mesh: row: 16 (over z, core), col: 16 (over y, x).
Axes of the slice: x: 4, y: 4, z: 8, core: 2. Of those that a mesh axis runs over, the one named last changes fastest.
Arguments:
- schur_blocks: bfloat16 [2, 16, 2, 16, 256, 256], P(None, 'row', None, 'col'), may hold values from -0.1875 to 0.1875
- known_blocks: float32 [2, 16, 2, 16, 256, 256], P(None, 'row', None, 'col'), may hold values from -6 to 6
- eigen_pairs: float32 [2, 16, 2, 256, 256], P(None, 'row'), as said below
- eigenvalues: float32 [32, 256], replicated, may hold values from 1 to 8.95, as said below
Outputs:
- updated: float32 [2, 16, 2, 16, 256, 256], P(None, 'row', None, 'col')
Inputs may be any that keep to these rules, and one draw needn't show every extreme that they name: For each block, eigen_pairs[a, r, 0] is unit upper triangular and eigen_pairs[a, r, 1] is its inverse. `eigenvalues`: row i lies within 1 + i / 4 and 1.2 + i / 4.
All inputs are finite; a program needn't handle non-finite values.
Results may differ from a plain program's by a relative error of at most 0.0017.
Values may be sent and summed in bfloat16 or wider, within the bound.
A program may use at most 128 MiB of HBM per device.

v0:
```python
import jax
import jax.numpy as jnp
from jax import lax
from jax.sharding import PartitionSpec as P

FIRST = 8
DIAGS = 4


def side_by_side(arrays, axis, dim, along):
    both = jnp.concatenate(arrays, axis=along)
    whole, at, outs = (lax.all_gather(both, axis, axis=dim, tiled=True), 0, [])
    for a in arrays:
        outs.append(lax.slice_in_dim(whole, at, at + a.shape[along], axis=along))
        at += a.shape[along]
    return tuple(outs)


def shifted(block, axis, distance):
    devices = range(lax.axis_size(axis))
    route = [((i - distance) % len(devices), i) for i in devices]
    return lax.ppermute(block, axis, route)


def pick_rows(stacked, indices):
    return jax.vmap(lambda source, chosen: source[chosen])(stacked, indices)


def full_dot(left_side, right_side):
    return jnp.einsum(
        "apq,aqr->apr",
        left_side,
        right_side,
        precision=lax.Precision.HIGHEST,
        preferred_element_type=jnp.float32,
    )


def right_terms(known_rows, schur_rows, known_cols, schur_cols, offsets, usable, distance):
    band_width = known_rows.shape[1]
    reach_back = distance[:, :, None] - offsets
    first_mask = usable & (offsets >= 1) & (reach_back >= 0) & (reach_back <= FIRST - 1)
    second_mask = usable & (offsets <= FIRST - 1) & (reach_back >= 1)
    clipped = jnp.clip(reach_back, 0, band_width - 1)
    known_pick = jnp.where(first_mask[..., None, None], pick_rows(known_rows, clipped), 0)
    schur_pick = jnp.where(second_mask[..., None, None], -pick_rows(schur_rows, clipped), 0)
    left_side = jnp.concatenate([known_pick, schur_pick], axis=2)
    right_side = jnp.concatenate([schur_cols, known_cols], axis=2)
    return jnp.einsum(
        "atepq,ateqr->atpr", left_side, right_side, preferred_element_type=jnp.float32
    )


def body(schur_blocks, known_blocks, eigen_pairs, eigenvalues):
    row_count = lax.axis_size("row")
    col_count = lax.axis_size("col")
    row_index = lax.axis_index("row")
    col_index = lax.axis_index("col")
    schur_local = schur_blocks[:, 0, :, 0]
    known_local = known_blocks[:, 0, :, 0]
    pairs_local = eigen_pairs[:, 0]
    block_rows = schur_local.shape[0]
    block_cols = schur_local.shape[1]
    blocks_total = block_rows * row_count
    band_width = FIRST + DIAGS
    row_slots = -(-band_width // col_count)
    col_slots = -(-band_width // row_count)
    per_row = -(-DIAGS // col_count)
    row_ids = jnp.arange(block_rows, dtype=jnp.int32) * row_count + row_index
    col_ids = jnp.arange(block_cols, dtype=jnp.int32) * col_count + col_index
    band_range = jnp.arange(band_width, dtype=jnp.int32)
    row_range = jnp.arange(block_rows, dtype=jnp.int32)
    row_offsets = (
        jnp.mod(col_index - row_ids, col_count)[:, None]
        + jnp.arange(row_slots, dtype=jnp.int32)[None, :] * col_count
    )
    row_reach = row_ids[:, None] + row_offsets
    row_valid = (row_offsets < band_width) & (row_reach < blocks_total)
    row_pick = jnp.clip(row_reach // col_count, 0, block_cols - 1)
    known_send = jnp.where(
        row_valid[..., None, None], pick_rows(known_local, row_pick), 0.0
    ).astype(jnp.bfloat16)
    schur_send = jnp.where(row_valid[..., None, None], pick_rows(schur_local, row_pick), 0)
    known_recv, schur_recv = side_by_side((known_send[None], schur_send[None]), "col", 0, 1)
    row_source = jnp.mod(row_ids[:, None] + band_range[None, :], col_count)
    row_slot = (band_range // col_count)[None, :]
    known_rows = known_recv[row_source, row_range[:, None], row_slot]
    schur_rows = schur_recv[row_source, row_range[:, None], row_slot]
    col_offsets = (
        jnp.mod(col_ids - row_index, row_count)[:, None]
        + jnp.arange(col_slots, dtype=jnp.int32)[None, :] * row_count
    )
    col_reach = col_ids[:, None] - col_offsets
    col_valid = (col_offsets < band_width) & (col_reach >= 0)
    col_pick = jnp.clip(col_reach // row_count, 0, block_rows - 1)
    known_down = jnp.where(
        col_valid[..., None, None], pick_rows(jnp.swapaxes(known_local, 0, 1), col_pick), 0.0
    ).astype(jnp.bfloat16)
    schur_down = jnp.where(
        col_valid[..., None, None], pick_rows(jnp.swapaxes(schur_local, 0, 1), col_pick), 0
    )
    target_first = -((col_index - row_ids - FIRST) // col_count)
    target_block = target_first[:, None] + jnp.arange(per_row, dtype=jnp.int32)[None, :]
    target_cols = target_block * col_count + col_index
    distance = target_cols - row_ids[:, None]
    active = (target_block < block_cols) & (distance <= FIRST + DIAGS - 1)
    target_clip = jnp.clip(target_block, 0, block_cols - 1)
    own_strip = jnp.stack([known_down, schur_down])
    collected = jnp.zeros((row_count,) + own_strip.shape, jnp.bfloat16)
    collected = collected.at[row_index].set(own_strip)
    reach_rows = min(row_count, band_width)
    carried = own_strip
    for step in range(1, reach_rows):
        carried = shifted(carried, "row", row_count - 1)
        collected = collected.at[jnp.mod(row_index + step, row_count)].set(carried)
    known_all = collected[:, 0]
    schur_all = collected[:, 1]
    col_source = jnp.mod(target_cols[:, :, None] - band_range[None, None, :], row_count)
    col_slot = (band_range // row_count)[None, None, :]
    known_cols = known_all[col_source, target_clip[:, :, None], col_slot]
    schur_cols = schur_all[col_source, target_clip[:, :, None], col_slot]
    offsets = jnp.broadcast_to(band_range[None, None, :], col_source.shape)
    totals = right_terms(
        known_rows,
        schur_rows,
        known_cols,
        schur_cols,
        offsets,
        jnp.ones(offsets.shape, jnp.bool_),
        distance,
    )
    kept_cols = schur_cols[:, :, :DIAGS]
    pair_list = []
    for distance_now in range(FIRST, FIRST + DIAGS):
        lag = distance_now % row_count
        receiver = jnp.mod(row_index - lag, row_count)
        wanted = jnp.clip(
            (row_range * row_count + receiver + distance_now) // row_count, 0, block_rows - 1
        )
        sending = pairs_local[wanted]
        pair_list.append(
            shifted(sending.astype(jnp.bfloat16), "row", row_count - lag).astype(sending.dtype)
        )
    vec_left = pairs_local[:, 0]
    inv_left = pairs_local[:, 1]
    lam_left = eigenvalues[row_ids]
    output = known_local
    for distance_now in range(FIRST, FIRST + DIAGS):
        hitting = active & (distance == distance_now)
        solving = jnp.any(hitting, axis=1)
        chosen = jnp.sum(jnp.where(hitting[..., None, None], totals, 0.0), axis=1)
        block_col = jnp.sum(jnp.where(hitting, target_clip, 0), axis=1)
        block_ids = jnp.clip(block_col * col_count + col_index, 0, blocks_total - 1)
        vec_right = pair_list[distance_now - FIRST][:, 0]
        inv_right = pair_list[distance_now - FIRST][:, 1]
        lam_right = eigenvalues[block_ids]
        spacing = lam_left[:, :, None] - lam_right[:, None, :]
        spacing = jnp.where(solving[:, None, None], spacing, 1.0)
        mixed_block = full_dot(full_dot(inv_left, chosen), vec_right) / spacing
        solved = full_dot(full_dot(vec_left, mixed_block), inv_right)
        solved = jnp.where(solving[:, None, None], solved, 0.0)
        placing = solving[:, None] & (
            jnp.arange(block_cols, dtype=jnp.int32)[None, :] == block_col[:, None]
        )
        output = jnp.where(placing[:, :, None, None], solved[:, None], output)
        if distance_now < FIRST + DIAGS - 1:
            rounded = solved.astype(jnp.bfloat16)
            for gap in range(1, FIRST + DIAGS - distance_now):
                row_new = shifted(rounded, "col", gap)
                receiver = jnp.mod(row_index - gap, row_count)
                wanted = jnp.clip(
                    (row_range * row_count + receiver + gap) // row_count, 0, block_rows - 1
                )
                col_new = shifted(rounded[wanted], "row", row_count - gap)
                growing = active & (distance - distance_now == gap)
                known_from_row = row_new[:, None]
                known_from_col = col_new[:, None]
                schur_from_row = schur_rows[:, gap][:, None]
                schur_from_col = kept_cols[:, :, gap]
                left_side = jnp.stack(
                    [
                        jnp.where(growing[..., None, None], known_from_row, 0),
                        jnp.where(growing[..., None, None], -schur_from_row, 0),
                    ],
                    axis=2,
                )
                right_side = jnp.stack([schur_from_col, known_from_col], axis=2)
                totals = totals + jnp.einsum(
                    "atepq,ateqr->atpr", left_side, right_side, preferred_element_type=jnp.float32
                )
    return output[:, None, :, None]


def solution(mesh):
    return jax.shard_map(
        body,
        mesh=mesh,
        in_specs=(
            P(None, "row", None, "col", None, None),
            P(None, "row", None, "col", None, None),
            P(None, "row", None, None, None),
            P(),
        ),
        out_specs=P(None, "row", None, "col", None, None),
        check_vma=False,
    )
```

profile of v0, /device:TPU:1, one launch (start us, length us, event | category | flops | bytes accessed | tf_op | source)
XLA Modules:
  0.0 308.4 jit_solution(7568952114232371289)
XLA Ops:
  16.7 6.5 %collective-permute-done = bf16[2,2,1,256,256]{4,3,2,1,0:T(8,128)(2,1)S(1)} collective-permute-done((bf16[2,2,1,256,256]{4,3,2,1,0:T(8,128)(2,1)S(1)}, bf16[2,2,1,256,256]{4,3,2,1,0:T(8,128)(2,1)S(1)}, u32[]{:S(2)}, u32[]{:S(2)}) %collective-permute-start) | collective-permute-done | bytes 524320 | tf_op jit(solution)/shard_map/ppermute | solution.py:22
  32.1 5.8 %collective-permute-start.18 = (bf16[2,2,256,256]{3,2,0,1:T(8,128)(2,1)}, bf16[2,2,256,256]{3,2,0,1:T(8,128)(2,1)}, u32[]{:S(2)}, u32[]{:S(2)}) collective-permute-start(bf16[2,2,256,256]{3,2,0,1:T(8,128)(2,1)} %copy.118), channel_id=1, source_target_pairs={{144,0},{160,16},{176,32},{192,48},{208,64},{224,80},{240,96},{0,1... | collective-permute-start | bytes 1572872 | tf_op jit(solution)/shard_map/ppermute | solution.py:22
  43.1 25.7 %collective-permute-start.2 = (bf16[2,2,1,256,256]{4,3,2,1,0:T(8,128)(2,1)}, bf16[2,2,1,256,256]{4,3,2,1,0:T(8,128)(2,1)S(1)}, u32[]{:S(2)}, u32[]{:S(2)}) collective-permute-start(bf16[2,2,1,256,256]{4,3,2,1,0:T(8,128)(2,1)} %collective-permute-done.1), channel_id=1, source_target_pairs={{16,0},{32,16},{48,32},{64,48},{80,64},{96,80},{112,96},{128,112},... | collective-permute-start | bytes 1572872 | tf_op jit(solution)/shard_map/ppermute | solution.py:22
  71.3 8.2 %collective-permute-start.3 = (bf16[2,2,1,256,256]{4,3,2,1,0:T(8,128)(2,1)S(1)}, bf16[2,2,1,256,256]{4,3,2,1,0:T(8,128)(2,1)S(1)}, u32[]{:S(2)}, u32[]{:S(2)}) collective-permute-start(bf16[2,2,1,256,256]{4,3,2,1,0:T(8,128)(2,1)S(1)} %collective-permute-done.2), channel_id=1, source_target_pairs={{16,0},{32,16},{48,32},{64,48},{80,64},{96,80},{112,96},{128,112},... | collective-permute-start | bytes 1572872 | tf_op jit(solution)/shard_map/ppermute | solution.py:22
  81.0 8.6 %collective-permute-start.4 = (bf16[2,2,1,256,256]{4,3,2,1,0:T(8,128)(2,1)S(1)}, bf16[2,2,1,256,256]{4,3,2,1,0:T(8,128)(2,1)S(1)}, u32[]{:S(2)}, u32[]{:S(2)}) collective-permute-start(bf16[2,2,1,256,256]{4,3,2,1,0:T(8,128)(2,1)S(1)} %collective-permute-done.3), channel_id=1, source_target_pairs={{16,0},{32,16},{48,32},{64,48},{80,64},{96,80},{112,96},{128,112},... | collective-permute-start | bytes 1572872 | tf_op jit(solution)/shard_map/ppermute | solution.py:22
  91.1 8.7 %collective-permute-start.5 = (bf16[2,2,1,256,256]{4,3,2,1,0:T(8,128)(2,1)S(1)}, bf16[2,2,1,256,256]{4,3,2,1,0:T(8,128)(2,1)S(1)}, u32[]{:S(2)}, u32[]{:S(2)}) collective-permute-start(bf16[2,2,1,256,256]{4,3,2,1,0:T(8,128)(2,1)S(1)} %collective-permute-done.4), channel_id=1, source_target_pairs={{16,0},{32,16},{48,32},{64,48},{80,64},{96,80},{112,96},{128,112},... | collective-permute-start | bytes 1572872 | tf_op jit(solution)/shard_map/ppermute | solution.py:22
  100.8 4.2 %broadcast_in_dim.425 = bf16[16,2,2,1,256,256]{5,4,2,1,3,0:T(8,128)(2,1)} broadcast(bf16[]{:T(256)} %constant.536.clone.1), dimensions={} | broadcast | bytes 8388610 | tf_op jit(solution)/shard_map/broadcast_in_dim | solution.py:109
  110.2 5.3 %collective-permute-done.6 = bf16[2,2,1,256,256]{4,3,2,1,0:T(8,128)(2,1)} collective-permute-done((bf16[2,2,1,256,256]{4,3,2,1,0:T(8,128)(2,1)S(1)}, bf16[2,2,1,256,256]{4,3,2,1,0:T(8,128)(2,1)}, u32[]{:S(2)}, u32[]{:S(2)}) %collective-permute-start.6) | collective-permute-done | bytes 524320 | tf_op jit(solution)/shard_map/ppermute | solution.py:22
  115.5 4.8 %collective-permute-start.7 = (bf16[2,2,1,256,256]{4,3,2,1,0:T(8,128)(2,1)}, bf16[2,2,1,256,256]{4,3,2,1,0:T(8,128)(2,1)}, u32[]{:S(2)}, u32[]{:S(2)}) collective-permute-start(bf16[2,2,1,256,256]{4,3,2,1,0:T(8,128)(2,1)} %collective-permute-done.6), channel_id=1, source_target_pairs={{16,0},{32,16},{48,32},{64,48},{80,64},{96,80},{112,96},{128,112},... | collective-permute-start | bytes 1572872 | tf_op jit(solution)/shard_map/ppermute | solution.py:22
  125.1 5.7 %collective-permute-start.8 = (bf16[2,2,1,256,256]{4,3,2,1,0:T(8,128)(2,1)}, bf16[2,2,1,256,256]{4,3,2,1,0:T(8,128)(2,1)S(1)}, u32[]{:S(2)}, u32[]{:S(2)}) collective-permute-start(bf16[2,2,1,256,256]{4,3,2,1,0:T(8,128)(2,1)} %collective-permute-done.7), channel_id=1, source_target_pairs={{16,0},{32,16},{48,32},{64,48},{80,64},{96,80},{112,96},{128,112},... | collective-permute-start | bytes 1572872 | tf_op jit(solution)/shard_map/ppermute | solution.py:22
  162.6 5.9 %slice_bitcast_fusion.1 = (bf16[16,2,1,256,256]{4,3,1,0,2:T(8,128)(2,1)}, bf16[16,2,1,256,256]{4,3,1,0,2:T(8,128)(2,1)}) fusion(bf16[16,2,2,1,256,256]{5,4,2,1,3,0:T(8,128)(2,1)} %fusion.30), kind=kLoop, calls=%fused_computation.33 | loop fusion | bytes 16777216 | tf_op jit(solution)/shard_map/squeeze | solution.py:117
  168.5 4.7 %gather_fusion.2 = bf16[24,256,256]{2,1,0:T(8,128)(2,1)} fusion(bf16[16,2,1,256,256]{4,3,1,0,2:T(8,128)(2,1)} %get-tuple-element.174, s32[24]{0:T(128)S(1)} %reshape.2426), kind=kCustom, calls=%fused_computation.2 | custom fusion | bytes 6291744 | tf_op jit(solution)/shard_map/gather | solution.py:121
  173.2 4.7 %gather_fusion.3 = bf16[24,256,256]{2,1,0:T(8,128)(2,1)} fusion(bf16[16,2,1,256,256]{4,3,1,0,2:T(8,128)(2,1)} %get-tuple-element.175, s32[24]{0:T(128)S(1)} %reshape.2426), kind=kCustom, calls=%fused_computation.3 | custom fusion | bytes 6291744 | tf_op jit(solution)/shard_map/gather | solution.py:120
  179.8 6.1 %fusion.123 = (bf16[16,2,1,256,256]{4,3,2,1,0:T(8,128)(2,1)}, bf16[16,2,1,256,256]{4,3,2,1,0:T(8,128)(2,1)}) fusion(bf16[16,4,1,256,256]{4,3,2,1,0:T(8,128)(2,1)} %all-gather.2.cloned.1.call-done), kind=kLoop, calls=%fused_computation.387 | loop fusion | bytes 16777216 | tf_op jit(solution)/shard_map/slice | solution.py:14
  185.9 4.7 %gather_fusion.1 = bf16[24,256,256]{2,1,0:T(8,128)(2,1)} fusion(bf16[16,2,1,256,256]{4,3,2,1,0:T(8,128)(2,1)} %get-tuple-element.173, s32[24]{0:T(128)S(1)} %reshape.2412), kind=kCustom, calls=%fused_computation.1 | custom fusion | bytes 6291744 | tf_op jit(solution)/shard_map/gather | solution.py:88
  190.6 4.4 %gather_fusion.22 = bf16[24,256,256]{2,1,0:T(8,128)(2,1)} fusion(bf16[2,12,256,256]{3,2,1,0:T(8,128)(2,1)} %bitcast.311, s32[24]{0:T(128)S(1)} %reshape.2578), kind=kCustom, calls=%fused_computation.22 | custom fusion | bytes 6291648 | tf_op jit(solution)/shard_map/vmap()/gather | solution.py:26
  195.0 4.3 %neg.157 = bf16[24,256,256]{2,1,0:T(8,128)(2,1)} negate(bf16[24,256,256]{2,1,0:T(8,128)(2,1)} %gather_fusion.22) | non-fusion elementwise | flops 1572864 | bytes 6291456 | tf_op jit(solution)/shard_map/neg | solution.py:46
  199.3 4.7 %gather_fusion = bf16[24,256,256]{2,1,0:T(8,128)(2,1)} fusion(bf16[16,2,1,256,256]{4,3,2,1,0:T(8,128)(2,1)} %get-tuple-element.172, s32[24]{0:T(128)S(1)} %reshape.2412), kind=kCustom, calls=%fused_computation | custom fusion | bytes 6291744 | tf_op jit(solution)/shard_map/gather | solution.py:87
  204.0 4.4 %gather_fusion.21 = bf16[24,256,256]{2,1,0:T(8,128)(2,1)} fusion(bf16[2,12,256,256]{3,2,1,0:T(8,128)(2,1)} %bitcast.315, s32[24]{0:T(128)S(1)} %reshape.2578), kind=kCustom, calls=%fused_computation.21 | custom fusion | bytes 6291648 | tf_op jit(solution)/shard_map/vmap()/gather | solution.py:26
  239.0 4.9 %collective-permute-done.16 = bf16[2,256,256]{2,1,0:T(8,128)(2,1)S(1)} collective-permute-done((bf16[2,256,256]{2,1,0:T(8,128)(2,1)S(1)}, bf16[2,256,256]{2,1,0:T(8,128)(2,1)S(1)}, u32[]{:S(2)}, u32[]{:S(2)}) %collective-permute-start.16) | collective-permute-done | bytes 262176 | tf_op jit(solution)/shard_map/ppermute | solution.py:22
  244.0 4.1 %collective-permute-done.17 = bf16[2,256,256]{2,1,0:T(8,128)(2,1)S(1)} collective-permute-done((bf16[2,256,256]{2,1,0:T(8,128)(2,1)}, bf16[2,256,256]{2,1,0:T(8,128)(2,1)S(1)}, u32[]{:S(2)}, u32[]{:S(2)}) %collective-permute-start.17) | collective-permute-done | bytes 262176 | tf_op jit(solution)/shard_map/ppermute | solution.py:22
  249.4 4.3 %collective-permute-done.12 = bf16[2,256,256]{2,1,0:T(8,128)(2,1)S(1)} collective-permute-done((bf16[2,256,256]{2,1,0:T(8,128)(2,1)S(1)}, bf16[2,256,256]{2,1,0:T(8,128)(2,1)S(1)}, u32[]{:S(2)}, u32[]{:S(2)}) %collective-permute-start.12) | collective-permute-done | bytes 262176 | tf_op jit(solution)/shard_map/ppermute | solution.py:22
  272.8 4.3 %collective-permute-done.19 = bf16[2,256,256]{2,1,0:T(8,128)(2,1)S(1)} collective-permute-done((bf16[2,256,256]{2,1,0:T(8,128)(2,1)S(1)}, bf16[2,256,256]{2,1,0:T(8,128)(2,1)S(1)}, u32[]{:S(2)}, u32[]{:S(2)}) %collective-permute-start.19) | collective-permute-done | bytes 262176 | tf_op jit(solution)/shard_map/ppermute | solution.py:22
  286.0 8.6 %collective-permute-done.24 = bf16[2,256,256]{2,1,0:T(8,128)(2,1)S(1)} collective-permute-done((bf16[2,256,256]{2,1,0:T(8,128)(2,1)}, bf16[2,256,256]{2,1,0:T(8,128)(2,1)S(1)}, u32[]{:S(2)}, u32[]{:S(2)}) %collective-permute-start.24) | collective-permute-done | bytes 262176 | tf_op jit(solution)/shard_map/ppermute | solution.py:22
  (216 shorter events, 140.8 us)
Async XLA Ops:
  6.5 173.3 %all-gather.2.cloned.1.call-start = ((), (), s32[]{:S(2)}) async-start(), calls=%async_computation | async-start | bytes 8912896 | tf_op jit(solution)/shard_map/all_gather | solution.py:12
  13.3 9.9 %collective-permute-start = (bf16[2,2,1,256,256]{4,3,2,1,0:T(8,128)(2,1)S(1)}, bf16[2,2,1,256,256]{4,3,2,1,0:T(8,128)(2,1)S(1)}, u32[]{:S(2)}, u32[]{:S(2)}) collective-permute-start(bf16[2,2,1,256,256]{4,3,2,1,0:T(8,128)(2,1)S(1)} %pad_maximum_fusion.6), channel_id=1, source_target_pairs={{16,0},{32,16},{48,32},{64,48},{80,64},{96,80},{112,96},{128,112},... | collective-permute-start | bytes 1572872 | tf_op jit(solution)/shard_map/ppermute | solution.py:22
  23.2 19.8 %collective-permute-start.1 = (bf16[2,2,1,256,256]{4,3,2,1,0:T(8,128)(2,1)S(1)}, bf16[2,2,1,256,256]{4,3,2,1,0:T(8,128)(2,1)}, u32[]{:S(2)}, u32[]{:S(2)}) collective-permute-start(bf16[2,2,1,256,256]{4,3,2,1,0:T(8,128)(2,1)S(1)} %collective-permute-done), channel_id=1, source_target_pairs={{16,0},{32,16},{48,32},{64,48},{80,64},{96,80},{112,96},{128,112},... | collective-permute-start | bytes 1572872 | tf_op jit(solution)/shard_map/ppermute | solution.py:22
  27.5 191.5 %collective-permute-start.11 = (bf16[2,2,256,256]{3,2,0,1:T(8,128)(2,1)S(1)}, bf16[2,2,256,256]{3,2,0,1:T(8,128)(2,1)}, u32[]{:S(2)}, u32[]{:S(2)}) collective-permute-start(bf16[2,2,256,256]{3,2,0,1:T(8,128)(2,1)S(1)} %copy.119), channel_id=1, source_target_pairs={{128,0},{144,16},{160,32},{176,48},{192,64},{208,80},{224,96},{240... | collective-permute-start | bytes 1572872 | tf_op jit(solution)/shard_map/ppermute | solution.py:22
  32.1 223.4 %collective-permute-start.18 = (bf16[2,2,256,256]{3,2,0,1:T(8,128)(2,1)}, bf16[2,2,256,256]{3,2,0,1:T(8,128)(2,1)}, u32[]{:S(2)}, u32[]{:S(2)}) collective-permute-start(bf16[2,2,256,256]{3,2,0,1:T(8,128)(2,1)} %copy.118), channel_id=1, source_target_pairs={{144,0},{160,16},{176,32},{192,48},{208,64},{224,80},{240,96},{0,1... | collective-permute-start | bytes 1572872 | tf_op jit(solution)/shard_map/ppermute | solution.py:22
  39.5 239.7 %collective-permute-start.23 = (bf16[2,2,256,256]{3,2,0,1:T(8,128)(2,1)}, bf16[2,2,256,256]{3,2,0,1:T(8,128)(2,1)}, u32[]{:S(2)}, u32[]{:S(2)}) collective-permute-start(bf16[2,2,256,256]{3,2,0,1:T(8,128)(2,1)} %copy.117), channel_id=1, source_target_pairs={{160,0},{176,16},{192,32},{208,48},{224,64},{240,80},{0,96},{16,11... | collective-permute-start | bytes 1572872 | tf_op jit(solution)/shard_map/ppermute | solution.py:22
  41.1 255.6 %collective-permute-start.26 = (bf16[2,2,256,256]{3,2,0,1:T(8,128)(2,1)}, bf16[2,2,256,256]{3,2,0,1:T(8,128)(2,1)}, u32[]{:S(2)}, u32[]{:S(2)}) collective-permute-start(bf16[2,2,256,256]{3,2,0,1:T(8,128)(2,1)} %copy.116), channel_id=1, source_target_pairs={{176,0},{192,16},{208,32},{224,48},{240,64},{0,80},{16,96},{32,112... | collective-permute-start | bytes 1572872 | tf_op jit(solution)/shard_map/ppermute | solution.py:22
  43.1 28.2 %collective-permute-start.2 = (bf16[2,2,1,256,256]{4,3,2,1,0:T(8,128)(2,1)}, bf16[2,2,1,256,256]{4,3,2,1,0:T(8,128)(2,1)S(1)}, u32[]{:S(2)}, u32[]{:S(2)}) collective-permute-start(bf16[2,2,1,256,256]{4,3,2,1,0:T(8,128)(2,1)} %collective-permute-done.1), channel_id=1, source_target_pairs={{16,0},{32,16},{48,32},{64,48},{80,64},{96,80},{112,96},{128,112},... | collective-permute-start | bytes 1572872 | tf_op jit(solution)/shard_map/ppermute | solution.py:22
  71.3 9.7 %collective-permute-start.3 = (bf16[2,2,1,256,256]{4,3,2,1,0:T(8,128)(2,1)S(1)}, bf16[2,2,1,256,256]{4,3,2,1,0:T(8,128)(2,1)S(1)}, u32[]{:S(2)}, u32[]{:S(2)}) collective-permute-start(bf16[2,2,1,256,256]{4,3,2,1,0:T(8,128)(2,1)S(1)} %collective-permute-done.2), channel_id=1, source_target_pairs={{16,0},{32,16},{48,32},{64,48},{80,64},{96,80},{112,96},{128,112},... | collective-permute-start | bytes 1572872 | tf_op jit(solution)/shard_map/ppermute | solution.py:22
  81.0 10.1 %collective-permute-start.4 = (bf16[2,2,1,256,256]{4,3,2,1,0:T(8,128)(2,1)S(1)}, bf16[2,2,1,256,256]{4,3,2,1,0:T(8,128)(2,1)S(1)}, u32[]{:S(2)}, u32[]{:S(2)}) collective-permute-start(bf16[2,2,1,256,256]{4,3,2,1,0:T(8,128)(2,1)S(1)} %collective-permute-done.3), channel_id=1, source_target_pairs={{16,0},{32,16},{48,32},{64,48},{80,64},{96,80},{112,96},{128,112},... | collective-permute-start | bytes 1572872 | tf_op jit(solution)/shard_map/ppermute | solution.py:22
  91.1 15.4 %collective-permute-start.5 = (bf16[2,2,1,256,256]{4,3,2,1,0:T(8,128)(2,1)S(1)}, bf16[2,2,1,256,256]{4,3,2,1,0:T(8,128)(2,1)S(1)}, u32[]{:S(2)}, u32[]{:S(2)}) collective-permute-start(bf16[2,2,1,256,256]{4,3,2,1,0:T(8,128)(2,1)S(1)} %collective-permute-done.4), channel_id=1, source_target_pairs={{16,0},{32,16},{48,32},{64,48},{80,64},{96,80},{112,96},{128,112},... | collective-permute-start | bytes 1572872 | tf_op jit(solution)/shard_map/ppermute | solution.py:22
  115.5 9.6 %collective-permute-start.7 = (bf16[2,2,1,256,256]{4,3,2,1,0:T(8,128)(2,1)}, bf16[2,2,1,256,256]{4,3,2,1,0:T(8,128)(2,1)}, u32[]{:S(2)}, u32[]{:S(2)}) collective-permute-start(bf16[2,2,1,256,256]{4,3,2,1,0:T(8,128)(2,1)} %collective-permute-done.6), channel_id=1, source_target_pairs={{16,0},{32,16},{48,32},{64,48},{80,64},{96,80},{112,96},{128,112},... | collective-permute-start | bytes 1572872 | tf_op jit(solution)/shard_map/ppermute | solution.py:22
  125.1 13.7 %collective-permute-start.8 = (bf16[2,2,1,256,256]{4,3,2,1,0:T(8,128)(2,1)}, bf16[2,2,1,256,256]{4,3,2,1,0:T(8,128)(2,1)S(1)}, u32[]{:S(2)}, u32[]{:S(2)}) collective-permute-start(bf16[2,2,1,256,256]{4,3,2,1,0:T(8,128)(2,1)} %collective-permute-done.7), channel_id=1, source_target_pairs={{16,0},{32,16},{48,32},{64,48},{80,64},{96,80},{112,96},{128,112},... | collective-permute-start | bytes 1572872 | tf_op jit(solution)/shard_map/ppermute | solution.py:22
  138.8 11.4 %collective-permute-start.9 = (bf16[2,2,1,256,256]{4,3,2,1,0:T(8,128)(2,1)S(1)}, bf16[2,2,1,256,256]{4,3,2,1,0:T(8,128)(2,1)S(1)}, u32[]{:S(2)}, u32[]{:S(2)}) collective-permute-start(bf16[2,2,1,256,256]{4,3,2,1,0:T(8,128)(2,1)S(1)} %collective-permute-done.8), channel_id=1, source_target_pairs={{16,0},{32,16},{48,32},{64,48},{80,64},{96,80},{112,96},{128,112},... | collective-permute-start | bytes 1572872 | tf_op jit(solution)/shard_map/ppermute | solution.py:22
  150.1 9.9 %collective-permute-start.10 = (bf16[2,2,1,256,256]{4,3,2,1,0:T(8,128)(2,1)S(1)}, bf16[2,2,1,256,256]{4,3,2,1,0:T(8,128)(2,1)S(1)}, u32[]{:S(2)}, u32[]{:S(2)}) collective-permute-start(bf16[2,2,1,256,256]{4,3,2,1,0:T(8,128)(2,1)S(1)} %collective-permute-done.9), channel_id=1, source_target_pairs={{16,0},{32,16},{48,32},{64,48},{80,64},{96,80},{112,96},{128,112},... | collective-permute-start | bytes 1572872 | tf_op jit(solution)/shard_map/ppermute | solution.py:22
  222.4 12.1 %collective-permute-start.14 = (bf16[2,256,256]{2,1,0:T(8,128)(2,1)S(1)}, bf16[2,256,256]{2,1,0:T(8,128)(2,1)}, u32[]{:S(2)}, u32[]{:S(2)}) collective-permute-start(bf16[2,256,256]{2,1,0:T(8,128)(2,1)S(1)} %get-tuple-element.207), channel_id=1, source_target_pairs={{14,0},{15,1},{0,2},{1,3},{2,4},{3,5},{4,6},{5,7},{6,8},{7,9},{8,1... | collective-permute-start | bytes 786440 | tf_op jit(solution)/shard_map/ppermute | solution.py:22
  226.5 10.5 %collective-permute-start.15 = (bf16[2,256,256]{2,1,0:T(8,128)(2,1)}, bf16[2,256,256]{2,1,0:T(8,128)(2,1)}, u32[]{:S(2)}, u32[]{:S(2)}) collective-permute-start(bf16[2,256,256]{2,1,0:T(8,128)(2,1)} %gather_fusion.8), channel_id=1, source_target_pairs={{32,0},{48,16},{64,32},{80,48},{96,64},{112,80},{128,96},{144,112}... | collective-permute-start | bytes 786440 | tf_op jit(solution)/shard_map/ppermute | solution.py:22
  237.0 11.2 %collective-permute-start.17 = (bf16[2,256,256]{2,1,0:T(8,128)(2,1)}, bf16[2,256,256]{2,1,0:T(8,128)(2,1)S(1)}, u32[]{:S(2)}, u32[]{:S(2)}) collective-permute-start(bf16[2,256,256]{2,1,0:T(8,128)(2,1)} %gather_fusion.9), channel_id=1, source_target_pairs={{48,0},{64,16},{80,32},{96,48},{112,64},{128,80},{144,96},{160,112... | collective-permute-start | bytes 786440 | tf_op jit(solution)/shard_map/ppermute | solution.py:22
  243.9 9.8 %collective-permute-start.12 = (bf16[2,256,256]{2,1,0:T(8,128)(2,1)S(1)}, bf16[2,256,256]{2,1,0:T(8,128)(2,1)S(1)}, u32[]{:S(2)}, u32[]{:S(2)}) collective-permute-start(bf16[2,256,256]{2,1,0:T(8,128)(2,1)S(1)} %get-tuple-element.207), channel_id=1, source_target_pairs={{15,0},{0,1},{1,2},{2,3},{3,4},{4,5},{5,6},{6,7},{7,8},{8,9},{9,10... | collective-permute-start | bytes 786440 | tf_op jit(solution)/shard_map/ppermute | solution.py:22
  258.9 10.0 %collective-permute-start.21 = (bf16[2,256,256]{2,1,0:T(8,128)(2,1)S(1)}, bf16[2,256,256]{2,1,0:T(8,128)(2,1)S(1)}, u32[]{:S(2)}, u32[]{:S(2)}) collective-permute-start(bf16[2,256,256]{2,1,0:T(8,128)(2,1)S(1)} %get-tuple-element.209), channel_id=1, source_target_pairs={{14,0},{15,1},{0,2},{1,3},{2,4},{3,5},{4,6},{5,7},{6,8},{7,9},{8,1... | collective-permute-start | bytes 786440 | tf_op jit(solution)/shard_map/ppermute | solution.py:22
  261.6 9.8 %collective-permute-start.22 = (bf16[2,256,256]{2,1,0:T(8,128)(2,1)}, bf16[2,256,256]{2,1,0:T(8,128)(2,1)}, u32[]{:S(2)}, u32[]{:S(2)}) collective-permute-start(bf16[2,256,256]{2,1,0:T(8,128)(2,1)} %gather_fusion.13), channel_id=1, source_target_pairs={{32,0},{48,16},{64,32},{80,48},{96,64},{112,80},{128,96},{144,112}... | collective-permute-start | bytes 786440 | tf_op jit(solution)/shard_map/ppermute | solution.py:22
  266.2 11.0 %collective-permute-start.19 = (bf16[2,256,256]{2,1,0:T(8,128)(2,1)S(1)}, bf16[2,256,256]{2,1,0:T(8,128)(2,1)S(1)}, u32[]{:S(2)}, u32[]{:S(2)}) collective-permute-start(bf16[2,256,256]{2,1,0:T(8,128)(2,1)S(1)} %get-tuple-element.209), channel_id=1, source_target_pairs={{15,0},{0,1},{1,2},{2,3},{3,4},{4,5},{5,6},{6,7},{7,8},{8,9},{9,10... | collective-permute-start | bytes 786440 | tf_op jit(solution)/shard_map/ppermute | solution.py:22
  283.5 11.1 %collective-permute-start.24 = (bf16[2,256,256]{2,1,0:T(8,128)(2,1)}, bf16[2,256,256]{2,1,0:T(8,128)(2,1)S(1)}, u32[]{:S(2)}, u32[]{:S(2)}) collective-permute-start(bf16[2,256,256]{2,1,0:T(8,128)(2,1)} %get-tuple-element.211), channel_id=1, source_target_pairs={{15,0},{0,1},{1,2},{2,3},{3,4},{4,5},{5,6},{6,7},{7,8},{8,9},{9,10... | collective-permute-start | bytes 786440 | tf_op jit(solution)/shard_map/ppermute | solution.py:22
  285.1 9.6 %collective-permute-start.25 = (bf16[2,256,256]{2,1,0:T(8,128)(2,1)S(1)}, bf16[2,256,256]{2,1,0:T(8,128)(2,1)}, u32[]{:S(2)}, u32[]{:S(2)}) collective-permute-start(bf16[2,256,256]{2,1,0:T(8,128)(2,1)S(1)} %gather_fusion.16), channel_id=1, source_target_pairs={{16,0},{32,16},{48,32},{64,48},{80,64},{96,80},{112,96},{128,112},... | collective-permute-start | bytes 786440 | tf_op jit(solution)/shard_map/ppermute | solution.py:22
  (22 other events, 334.3 us)
Sparse Core Ops, SparseCore 0:
  10.6 79.4 all-gather.1
where the time goes:
time: 310 us; the launch traced here: 308 us
  starting transfers between devices  102 us (33%)
  local copies, waits for them, and re-layouts  69.7 us (22%)
  other arithmetic  48.6 us (16%)
  waiting for transfers between devices  46.4 us (15%)
  matrix products  27.5 us (9%)
  between operations  14.1 us (5%)
    ppermute x27, starting transfers between devices, shifted(): return lax.ppermute(block, axis, route)  102 us
    ppermute x27, waiting for transfers between devices, shifted(): return lax.ppermute(block, axis, route)  46.3 us
    scatter x11, other arithmetic, body(): collected = collected.at[jnp.mod(row_index + step, row_count)].set(carried)  29.1 us
    dot_general x16, matrix products, full_dot(): jnp.einsum('apq,aqr->apr', left_side, right_side, precision=lax.Precision...  17.2 us
    gather x8, local copies, waits for them, and re-layouts, pick_rows(): return jax.vmap(lambda source, chosen: source[chosen])(stacked, indices)  13.8 us
    gather x6, local copies, waits for them, and re-layouts, body(): col_new = shifted(rounded[wanted], 'row', row_count - gap)  7.84 us
    dot_general x6, matrix products, body(): jnp.einsum('atepq,ateqr->atpr', left_side, right_side, preferred_element_...  6.89 us
  transfers between devices with their start and end apart: 28, of which 12 were waited for; matrix products, arithmetic and copies ran while one was open for 44% of the time, Pallas kernels for 0%

commit v1 on v0

v1 whole, which is shorter than its diff:
```python
import functools

import jax
import jax.numpy as jnp
from jax import lax
from jax.experimental import pallas as pl
from jax.experimental.pallas import tpu as pltpu
from jax.sharding import PartitionSpec as P

FIRST = 8
DIAGS = 4
SIDE = 16
TOTAL = 32
MESH = pl.DeviceIdType.MESH


def remote(src, dst, send_sem, recv_sem, row, col):
    return pltpu.make_async_remote_copy(
        src_ref=src, dst_ref=dst, send_sem=send_sem, recv_sem=recv_sem,
        device_id=(row, col), device_id_type=MESH,
    )


def arrived(ref, sem):
    pltpu.make_async_copy(ref, ref, sem).wait()


def wrap(x):
    return lax.rem(x + 2 * SIDE, SIDE)


def dot(a, b):
    return jnp.dot(a, b, preferred_element_type=jnp.float32)


def halves(x):
    high = x.astype(jnp.bfloat16)
    return high, (x - high.astype(jnp.float32)).astype(jnp.bfloat16)


def left_dot(a, x):
    high, low = halves(x)
    return dot(a, high) + dot(a, low)


def right_dot(x, b):
    high, low = halves(x)
    return dot(high, b) + dot(low, b)


def kernel(
    schur, known, pairs, lam, out,
    row_f, row_s, col_f, col_s, vj, new_r, new_c, total, gap, fresh,
    q_row_f, q_row_s, q_col_f, q_col_s, q_vj, q_new_r, q_new_c,
    s_src, s_ring_f, s_ring_s, s_chain_f, s_chain_s, s_chain_v, s_own, s_new,
):
    r = lax.axis_index("row")
    c = lax.axis_index("col")
    e = wrap(c - r)
    m = e - FIRST
    is_target = (e >= FIRST) & (e < FIRST + DIAGS)
    later = []

    def send(cond, *args):
        copy = remote(*args)

        @pl.when(cond)
        def _():
            copy.start()

        later.append((cond, copy))

    barrier = pltpu.get_barrier_semaphore()

    def greet(step, carry):
        pl.semaphore_signal(barrier, inc=1, device_id=(wrap(r + step), c), device_id_type=MESH)
        pl.semaphore_signal(barrier, inc=1, device_id=(r, wrap(c + step)), device_id_type=MESH)
        return carry

    lax.fori_loop(1, SIDE, greet, 0)
    pl.semaphore_wait(barrier, 2 * (SIDE - 1))

    near = e < FIRST
    eb = jnp.minimum(e, FIRST - 1)
    col_to = wrap(r + FIRST + lax.rem(e, DIAGS))
    places = []
    for t in (0, 1):
        k = r + SIDE * t
        j = k + e
        b = jnp.minimum(j // SIDE, 1)
        to_row = near & (k < TOTAL - FIRST)
        to_col = near & (j >= FIRST) & (j < TOTAL)
        last = jnp.minimum(DIAGS - 1, j - FIRST)
        i_to = j - FIRST - jnp.where(e >= DIAGS, 0, last)
        places.append((b, to_row, to_col, wrap(i_to), jnp.clip(i_to // SIDE, 0, 1)))
    for n, (ref, row_ref, col_ref, q_row, q_col) in enumerate(
        ((known, row_f, col_f, q_row_f, q_col_f), (schur, row_s, col_s, q_row_s, q_col_s))
    ):
        for t in (0, 1):
            b, to_row, to_col, row_to, t_to = places[t]
            used = e >= n
            send(to_row & used, ref.at[t, b], row_ref.at[t, eb], s_src.at[t, 2 * n], q_row.at[t, eb], r, col_to)
            send(to_col & used, ref.at[t, b], col_ref.at[t_to, eb], s_src.at[t, 2 * n + 1], q_col.at[t_to, eb], row_to, c)
    for t in (0, 1):
        b, to_row, to_col, row_to, t_to = places[t]
        send(to_col & (e == 0), pairs.at[t], vj.at[t_to], s_src.at[t, 4], q_vj.at[t_to], row_to, c)

    mb = jnp.clip(m, 0, DIAGS - 1)
    col_plus = wrap(r + FIRST + lax.rem(mb + 1, DIAGS))
    col_minus = wrap(r + FIRST + lax.rem(mb + DIAGS - 1, DIAGS))

    part, real, low_mem, high_mem = [], [], [], []
    for t in (0, 1):
        i = r + SIDE * t
        j = i + FIRST + m
        part.append(is_target & (i < TOTAL - FIRST))
        real.append(is_target & (j < TOTAL))
        low_mem.append(is_target & (j < TOTAL) & (m > 0))
        high_mem.append(is_target & (j < TOTAL) & (m < DIAGS - 1) & (i >= 1))

    def member(t, delta):
        i = r + SIDE * t - delta
        return wrap(i), jnp.clip(i // SIDE, 0, 1)

    for t in (0, 1):
        i = r + SIDE * t
        j = i + FIRST + m
        b = jnp.clip(j // SIDE, 0, 1)
        at = FIRST + mb

        @pl.when(real[t])
        def _():
            pltpu.make_async_copy(schur.at[t, b], row_s.at[t, at], q_row_s.at[t, at]).start()
            pltpu.make_async_copy(schur.at[t, b], col_s.at[t, at], q_col_s.at[t, at]).start()
            rows = jnp.broadcast_to(lam[pl.ds(i, 1), :], total.shape[1:]).T
            gap[t] = 1.0 / (rows - lam[pl.ds(jnp.clip(j, 0, TOTAL - 1), 1), :])
            total[t] = jnp.zeros(total.shape[1:], jnp.float32)

        for d in range(1, DIAGS):
            fits = real[t] & (m + d < DIAGS)
            send(fits & (j + d < TOTAL), schur.at[t, b], row_s.at[t, at], s_own.at[t, 0, d - 1], q_row_s.at[t, at], r, wrap(c + d))
            row_to, t_to = member(t, d)
            send(fits & (i >= d), schur.at[t, b], col_s.at[t_to, at], s_own.at[t, 1, d - 1], q_col_s.at[t_to, at], row_to, c)

    def ring_f(t, x, d):
        return remote(row_f.at[t, x], row_f.at[t, x], s_ring_f.at[t, x, d], q_row_f.at[t, x], r, (col_plus, col_minus)[d])

    def ring_s(t, x, d):
        return remote(row_s.at[t, x], row_s.at[t, x], s_ring_s.at[t, x, d], q_row_s.at[t, x], r, (col_plus, col_minus)[d])

    def chain_copy(t, x, ref, send_sems, recv_sems, up):
        row_to, t_to = member(t, 1 if up else -1)
        return remote(ref.at[t, x], ref.at[t_to, x], send_sems.at[t, x], recv_sems.at[t_to, x], row_to, c)

    def chain_v(t):
        row_to, t_to = member(t, -1)
        return remote(vj.at[t], vj.at[t_to], s_chain_v.at[t], q_vj.at[t_to], row_to, c)

    def ring_conds(t, x):
        away = lax.rem(mb - x + 2 * DIAGS, DIAGS)
        return away

    def accumulate(t, x):
        other = FIRST + mb - x
        total[t] += dot(row_f[t, other], col_s[t, x]) - dot(row_s[t, x], col_f[t, other])

    def run_if(cond, fn):
        pl.when(cond)(fn)

    def f_actions(t, x, what):
        away = ring_conds(t, x)
        run_if(part[t] & (away <= 1), lambda: what(ring_f(t, x, 0)))
        run_if(part[t] & (away == 0), lambda: what(ring_f(t, x, 1)))

    def s_actions(t, x, what):
        away = ring_conds(t, x)
        run_if(part[t] & (away == 0), lambda: what(ring_s(t, x, 0)))
        run_if(part[t] & ((away == 0) | (away == DIAGS - 1)), lambda: what(ring_s(t, x, 1)))

    def chain_actions(t, x, ref, send_sems, recv_sems, what):
        run_if(high_mem[t] & (x >= DIAGS), lambda: what(chain_copy(t, x, ref, send_sems, recv_sems, True)))
        run_if(low_mem[t] & (x < DIAGS), lambda: what(chain_copy(t, x, ref, send_sems, recv_sems, False)))

    def start(copy):
        copy.start()

    def sent(copy):
        copy.wait_send()

    def f_step(x, carry):
        for t in (0, 1):

            @pl.when(part[t])
            def _():
                arrived(row_f.at[t, x], q_row_f.at[t, x])

            f_actions(t, x, start)

            @pl.when(real[t])
            def _():
                arrived(col_f.at[t, x], q_col_f.at[t, x])

            chain_actions(t, x, col_f, s_chain_f, q_col_f, start)
        return carry

    lax.fori_loop(0, FIRST, f_step, 0)

    def s_step(x, carry):
        for t in (0, 1):

            @pl.when(part[t])
            def _():
                arrived(row_s.at[t, x], q_row_s.at[t, x])

            s_actions(t, x, start)

            @pl.when(real[t])
            def _():
                arrived(col_s.at[t, x], q_col_s.at[t, x])

            chain_actions(t, x, col_s, s_chain_s, q_col_s, start)
        for t in (0, 1):

            @pl.when(real[t] & (x > m))
            def _():
                accumulate(t, x)

        return carry

    lax.fori_loop(1, FIRST, s_step, 0)

    def far_step(x, carry):
        for t in (0, 1):

            @pl.when(real[t] & (x <= FIRST + m))
            def _():
                arrived(row_s.at[t, x], q_row_s.at[t, x])
                arrived(col_s.at[t, x], q_col_s.at[t, x])
                accumulate(t, x)

        return carry

    lax.fori_loop(FIRST, FIRST + DIAGS, far_step, 0)

    for t in (0, 1):

        @pl.when(real[t])
        def _():
            arrived(vj.at[t], q_vj.at[t])

        run_if(low_mem[t], lambda: start(chain_v(t)))

    for before in range(DIAGS - 1):
        for t in (0, 1):

            @pl.when(real[t] & (m > before))
            def _():
                near = jnp.clip(m - before, 1, DIAGS - 1)
                arrived(new_r.at[t, before], q_new_r.at[t, before])
                arrived(new_c.at[t, before], q_new_c.at[t, before])
                total[t] += dot(new_r[t, before], col_s[t, near]) - dot(row_s[t, near], new_c[t, before])

    @pl.when(is_target)
    def _():
        both = (0, 1)
        x = [left_dot(pairs[t, 1], total[t]) for t in both]
        x = [right_dot(x[t], vj[t, 0]) * gap[t] for t in both]
        x = [left_dot(pairs[t, 0], x[t]) for t in both]
        x = [right_dot(x[t], vj[t, 1]) for t in both]
        for t in both:
            fresh[t] = x[t].astype(jnp.bfloat16)
            out[t] = x[t]

    mb3 = jnp.minimum(mb, DIAGS - 2)
    for d in range(1, DIAGS):
        for t in (0, 1):
            i = r + SIDE * t
            fits = real[t] & (m + d < DIAGS)
            row_to, t_to = member(t, d)
            send(fits & (i + FIRST + m + d < TOTAL), fresh.at[t], new_r.at[t, mb3], s_new.at[t, 0, d - 1], q_new_r.at[t, mb3], r, wrap(c + d))
            send(fits & (i >= d), fresh.at[t], new_c.at[t_to, mb3], s_new.at[t, 1, d - 1], q_new_c.at[t_to, mb3], row_to, c)

    for cond, copy in later:
        run_if(cond, lambda: copy.wait_send())

    def drain(x, carry):
        for t in (0, 1):
            f_actions(t, x, sent)
            chain_actions(t, x, col_f, s_chain_f, q_col_f, sent)

            @pl.when(x >= 1)
            def _():
                s_actions(t, x, sent)
                chain_actions(t, x, col_s, s_chain_s, q_col_s, sent)

        return carry

    lax.fori_loop(0, FIRST, drain, 0)
    for t in (0, 1):
        run_if(low_mem[t], lambda: sent(chain_v(t)))


def exchange(schur, known, pairs, lam):
    bs = schur.shape[-1]
    half, full = jnp.bfloat16, jnp.float32
    dma = pltpu.SemaphoreType.DMA
    vmem = pl.BlockSpec(memory_space=pltpu.VMEM)
    return pl.pallas_call(
        kernel,
        out_shape=jax.ShapeDtypeStruct((2, bs, bs), full),
        in_specs=[vmem] * 4,
        out_specs=vmem,
        scratch_shapes=[
            pltpu.VMEM((2, FIRST, bs, bs), half),
            pltpu.VMEM((2, FIRST + DIAGS, bs, bs), half),
            pltpu.VMEM((2, FIRST, bs, bs), half),
            pltpu.VMEM((2, FIRST + DIAGS, bs, bs), half),
            pltpu.VMEM((2, 2, bs, bs), half),
            pltpu.VMEM((2, DIAGS - 1, bs, bs), half),
            pltpu.VMEM((2, DIAGS - 1, bs, bs), half),
            pltpu.VMEM((2, bs, bs), full),
            pltpu.VMEM((2, bs, bs), full),
            pltpu.VMEM((2, bs, bs), half),
            dma((2, FIRST)), dma((2, FIRST + DIAGS)), dma((2, FIRST)), dma((2, FIRST + DIAGS)),
            dma((2,)), dma((2, DIAGS - 1)), dma((2, DIAGS - 1)),
            dma((2, 5)), dma((2, FIRST, 2)), dma((2, FIRST, 2)), dma((2, FIRST)), dma((2, FIRST)),
            dma((2,)), dma((2, 2, DIAGS - 1)), dma((2, 2, DIAGS - 1)),
        ],
        compiler_params=pltpu.CompilerParams(
            collective_id=0, has_side_effects=True, vmem_limit_bytes=40 * 1024 * 1024
        ),
    )(schur, known, pairs, lam)


def body(schur_blocks, known_blocks, eigen_pairs, eigenvalues):
    known = known_blocks[:, 0, :, 0]
    solved = exchange(
        schur_blocks[:, 0, :, 0],
        known.astype(jnp.bfloat16),
        eigen_pairs[:, 0].astype(jnp.bfloat16),
        eigenvalues,
    )
    rows = lax.axis_index("row") + SIDE * jnp.arange(2)[:, None]
    cols = lax.axis_index("col") + SIDE * jnp.arange(2)[None, :]
    away = cols - rows
    new = (away >= FIRST) & (away < FIRST + DIAGS)
    output = jnp.where(new[:, :, None, None], solved[:, None], known)
    return output[:, None, :, None]


def solution(mesh):
    return jax.shard_map(
        body,
        mesh=mesh,
        in_specs=(
            P(None, "row", None, "col", None, None),
            P(None, "row", None, "col", None, None),
            P(None, "row", None, None, None),
            P(),
        ),
        out_specs=P(None, "row", None, "col", None, None),
        check_vma=False,
    )
```

time: 310 us -> 307 us (level)
  the two profiles are of different devices: /device:TPU:1 before, /device:TPU:22 now
where the time goes in v1:
time: 307 us
  Pallas kernels  303 us (99%)
    pallas_call x1, Pallas kernels, exchange(): pl.pallas_call(kernel, out_shape=jax.ShapeDtypeStruct((2, bs, bs), full),...  303 us

profile of v1, /device:TPU:22, one launch (start us, length us, event | category | flops | bytes accessed | tf_op | source)
XLA Modules:
  0.0 306.9 jit_solution(11313247669824229852)
XLA Ops:
  0.0 0.0 copy-start.2
  0.0 0.1 compare_and_fusion
  0.1 1.4 fusion.1.pairs
  1.4 0.1 copy-done.2
  1.5 0.0 copy-start
  1.5 0.0 copy-start.1
  1.5 0.1 fusion.known
  1.6 1.0 copy-done
  2.6 0.0 copy-done.1
  2.6 303.2 %shard_map.46 = f32[2,256,256]{2,1,0:T(8,128)S(1)} custom-call(bf16[2,2,256,256]{3,2,1,0:T(8,128)(2,1)S(1)} %bitcast.13, bf16[2,2,256,256]{3,2,1,0:T(8,128)(2,1)S(1)} %fusion.known, bf16[2,2,256,256]{3,2,1,0:T(8,128)(2,1)S(1)} %fusion.1.pairs, f32[32,256]{1,0:T(8,128)S(1)} %copy-done.1), custom_call_target="tpu_custom_call" | custom-call | tf_op jit(solution)/shard_map/pallas_call | solution.py:308
  305.8 1.1 broadcast_select_fusion
  (1 shorter events, 0.0 us)
Async XLA Ops:
  0.0 1.5 copy-start.2
  1.5 1.0 copy-start
  1.5 1.0 copy-start.1

commit v2 on v1

--- a/solution.py
+++ b/solution.py
@@ -156,10 +156,6 @@
         row_to, t_to = member(t, -1)
         return remote(vj.at[t], vj.at[t_to], s_chain_v.at[t], q_vj.at[t_to], row_to, c)
 
-    def ring_conds(t, x):
-        away = lax.rem(mb - x + 2 * DIAGS, DIAGS)
-        return away
-
     def accumulate(t, x):
         other = FIRST + mb - x
         total[t] += dot(row_f[t, other], col_s[t, x]) - dot(row_s[t, x], col_f[t, other])
@@ -167,88 +163,150 @@
     def run_if(cond, fn):
         pl.when(cond)(fn)
 
-    def f_actions(t, x, what):
-        away = ring_conds(t, x)
-        run_if(part[t] & (away <= 1), lambda: what(ring_f(t, x, 0)))
-        run_if(part[t] & (away == 0), lambda: what(ring_f(t, x, 1)))
-
-    def s_actions(t, x, what):
-        away = ring_conds(t, x)
-        run_if(part[t] & (away == 0), lambda: what(ring_s(t, x, 0)))
-        run_if(part[t] & ((away == 0) | (away == DIAGS - 1)), lambda: what(ring_s(t, x, 1)))
-
-    def chain_actions(t, x, ref, send_sems, recv_sems, what):
-        run_if(high_mem[t] & (x >= DIAGS), lambda: what(chain_copy(t, x, ref, send_sems, recv_sems, True)))
-        run_if(low_mem[t] & (x < DIAGS), lambda: what(chain_copy(t, x, ref, send_sems, recv_sems, False)))
-
-    def start(copy):
-        copy.start()
-
-    def sent(copy):
-        copy.wait_send()
-
-    def f_step(x, carry):
+    kinds = (
+        (row_f, q_row_f, ring_f, 0, col_f, s_chain_f, q_col_f),
+        (row_s, q_row_s, ring_s, 1, col_s, s_chain_s, q_col_s),
+    )
+
+    late0 = is_target & (r + e >= SIDE + FIRST)
+    t_col = (jnp.int32(0), jnp.where(real[1], 1, 0))
+    col_live = (real[0] & ~late0, real[1] | late0)
+
+    def place(n):
+        i = r + SIDE * t_col[n]
+        last = jnp.minimum(DIAGS - 1, i + m)
+        up = col_live[n] & (m < last)
+        down = col_live[n] & (m > 0)
+        return up, down, last - m
+
+    def row_entry(kind, t, start):
+        ref, sems, ring, dest = kind[0], kind[1], kind[2], kind[3]
+        for x in (mb, mb + DIAGS):
+
+            @pl.when(part[t] & (x >= dest))
+            def _():
+                if start:
+                    arrived(ref.at[t, x], sems.at[t, x])
+                    ring(t, x, 0).start()
+                    ring(t, x, 1).start()
+                else:
+                    ring(t, x, 0).wait_send()
+                    ring(t, x, 1).wait_send()
+
+    def row_relay(kind, t, start):
+        ref, sems, ring, dest = kind[0], kind[1], kind[2], kind[3]
+        base = lax.rem(mb + (1 if dest else DIAGS - 1), DIAGS)
+        for x in (base, base + DIAGS):
+
+            @pl.when(part[t] & (x >= dest))
+            def _():
+                if start:
+                    arrived(ref.at[t, x], sems.at[t, x])
+                    ring(t, x, dest).start()
+                else:
+                    ring(t, x, dest).wait_send()
+
+    def col_relay(kind, n, depths, start):
+        ref, send_sems, recv_sems = kind[4:]
+        up, down, from_last = place(n)
+        t = t_col[n]
+        up_now, down_now = jnp.bool_(False), jnp.bool_(False)
+        for depth in depths:
+            up_now |= up & (m == depth)
+            down_now |= down & (from_last == depth)
+
+        def step(x, carry):
+            @pl.when(up_now)
+            def _():
+                copy = chain_copy(t, x + DIAGS, ref, send_sems, recv_sems, True)
+                if start:
+                    arrived(ref.at[t, x + DIAGS], recv_sems.at[t, x + DIAGS])
+                    copy.start()
+                else:
+                    copy.wait_send()
+
+            @pl.when(down_now & (x >= kind[3]))
+            def _():
+                copy = chain_copy(t, x, ref, send_sems, recv_sems, False)
+                if start:
+                    arrived(ref.at[t, x], recv_sems.at[t, x])
+                    copy.start()
+                else:
+                    copy.wait_send()
+
+            return carry
+
+        lax.fori_loop(0, DIAGS, step, 0)
+
+    rounds = tuple((kind, n) for kind in kinds for n in (0, 1))
+
+    def first_hops(n):
+        kind, t = rounds[n]
+        row_entry(kind, t, True)
+        col_relay(kind, t, (0,), True)
+        col_relay(kind, t, (1,), True)
+
+    def second_hops(n):
+        kind, t = rounds[n]
+        row_relay(kind, t, True)
+        col_relay(kind, t, (2,), True)
+
+    for n in range(len(rounds)):
+        first_hops(n)
+        if n:
+            second_hops(n - 1)
+    second_hops(len(rounds) - 1)
+
+    up_of, down_of = [], []
+    for t in (0, 1):
+        last = jnp.minimum(DIAGS - 1, r + SIDE * t + m)
+        up_of.append(m < last)
+        down_of.append(m > 0)
+
+    def rest(x, carry):
+        away = lax.rem(mb - x + 2 * DIAGS, DIAGS)
         for t in (0, 1):
-
-            @pl.when(part[t])
-            def _():
-                arrived(row_f.at[t, x], q_row_f.at[t, x])
-
-            f_actions(t, x, start)
-
-            @pl.when(real[t])
-            def _():
-                arrived(col_f.at[t, x], q_col_f.at[t, x])
-
-            chain_actions(t, x, col_f, s_chain_f, q_col_f, start)
+            ends = jnp.where(x >= DIAGS, ~up_of[t], ~down_of[t])
+            run_if(part[t] & (away >= 2), lambda: arrived(row_f.at[t, x], q_row_f.at[t, x]))
+            run_if(real[t] & ends, lambda: arrived(col_f.at[t, x], q_col_f.at[t, x]))
+
+            @pl.when(x >= 1)
+            def _():
+                run_if(part[t] & ((away == 1) | (away == 2)), lambda: arrived(row_s.at[t, x], q_row_s.at[t, x]))
+                run_if(real[t] & ends, lambda: arrived(col_s.at[t, x], q_col_s.at[t, x]))
+
         return carry
 
-    lax.fori_loop(0, FIRST, f_step, 0)
-
-    def s_step(x, carry):
+    lax.fori_loop(0, FIRST, rest, 0)
+
+    def far(x, carry):
         for t in (0, 1):
 
-            @pl.when(part[t])
-            def _():
-                arrived(row_s.at[t, x], q_row_s.at[t, x])
-
-            s_actions(t, x, start)
-
-            @pl.when(real[t])
-            def _():
-                arrived(col_s.at[t, x], q_col_s.at[t, x])
-
-            chain_actions(t, x, col_s, s_chain_s, q_col_s, start)
-        for t in (0, 1):
-
-            @pl.when(real[t] & (x > m))
-            def _():
-                accumulate(t, x)
-
-        return carry
-
-    lax.fori_loop(1, FIRST, s_step, 0)
-
-    def far_step(x, carry):
-        for t in (0, 1):
-
-            @pl.when(real[t] & (x <= FIRST + m))
+            @pl.when(real[t] & (x >= FIRST) & (x <= FIRST + m))
             def _():
                 arrived(row_s.at[t, x], q_row_s.at[t, x])
                 arrived(col_s.at[t, x], q_col_s.at[t, x])
+
+            @pl.when(real[t] & (x > m) & (x <= FIRST + m))
+            def _():
                 accumulate(t, x)
 
         return carry
 
-    lax.fori_loop(FIRST, FIRST + DIAGS, far_step, 0)
-
-    for t in (0, 1):
-
-        @pl.when(real[t])
-        def _():
-            arrived(vj.at[t], q_vj.at[t])
-
-        run_if(low_mem[t], lambda: start(chain_v(t)))
+    lax.fori_loop(1, FIRST + DIAGS, far, 0)
+
+    for n in (0, 1):
+        _, down, from_last = place(n)
+        t = t_col[n]
+        for depth in range(DIAGS - 1):
+
+            @pl.when(down & (from_last == depth))
+            def _():
+                arrived(vj.at[t], q_vj.at[t])
+                chain_v(t).start()
+
+    for t in (0, 1):
+        run_if(real[t] & ~down_of[t], lambda: arrived(vj.at[t], q_vj.at[t]))
 
     for before in range(DIAGS - 1):
         for t in (0, 1):
@@ -283,21 +341,13 @@
     for cond, copy in later:
         run_if(cond, lambda: copy.wait_send())
 
-    def drain(x, carry):
-        for t in (0, 1):
-            f_actions(t, x, sent)
-            chain_actions(t, x, col_f, s_chain_f, q_col_f, sent)
-
-            @pl.when(x >= 1)
-            def _():
-                s_actions(t, x, sent)
-                chain_actions(t, x, col_s, s_chain_s, q_col_s, sent)
-
-        return carry
-
-    lax.fori_loop(0, FIRST, drain, 0)
-    for t in (0, 1):
-        run_if(low_mem[t], lambda: sent(chain_v(t)))
+    for kind, n in rounds:
+        row_entry(kind, n, False)
+        row_relay(kind, n, False)
+        col_relay(kind, n, (0, 1, 2), False)
+    for n in (0, 1):
+        _, down, _ = place(n)
+        run_if(down, lambda: chain_v(t_col[n]).wait_send())
 
 
 def exchange(schur, known, pairs, lam):

time: 307 us -> 124 us (0.40)
  the two profiles are of different devices: /device:TPU:22 before, /device:TPU:65 now
where the time goes in v2:
time: 124 us
  Pallas kernels  120 us (97%)
  other arithmetic  2.62 us (2%)
    pallas_call x1, Pallas kernels, exchange(): pl.pallas_call(kernel, out_shape=jax.ShapeDtypeStruct((2, bs, bs), full),...  120 us

profile of v2, /device:TPU:65, one launch (start us, length us, event | category | flops | bytes accessed | tf_op | source)
XLA Modules:
  0.0 123.8 jit_solution(4355914329711221337)
XLA Ops:
  0.0 0.0 copy-start.2
  0.0 0.1 compare_and_fusion
  0.1 1.4 %fusion.1.pairs = bf16[2,2,256,256]{3,2,1,0:T(8,128)(2,1)S(1)} fusion(f32[2,1,2,256,256]{4,3,2,1,0:T(8,128)} %param.6), kind=kLoop, calls=%fused_computation.3 | loop fusion | flops 262144 | bytes 1572864 | tf_op jit(solution)/shard_map/convert_element_type | solution.py:390
  1.4 0.1 copy-done.2
  1.5 0.0 copy-start
  1.5 0.0 copy-start.1
  1.5 0.1 fusion.known
  1.6 1.0 copy-done
  2.6 0.0 copy-done.1
  2.6 120.1 %shard_map.46 = f32[2,256,256]{2,1,0:T(8,128)S(1)} custom-call(bf16[2,2,256,256]{3,2,1,0:T(8,128)(2,1)S(1)} %bitcast.13, bf16[2,2,256,256]{3,2,1,0:T(8,128)(2,1)S(1)} %fusion.known, bf16[2,2,256,256]{3,2,1,0:T(8,128)(2,1)S(1)} %fusion.1.pairs, f32[32,256]{1,0:T(8,128)S(1)} %copy-done.1), custom_call_target="tpu_custom_call" | custom-call | tf_op jit(solution)/shard_map/pallas_call | solution.py:358
  122.7 1.1 broadcast_select_fusion
  (1 shorter events, 0.0 us)
Async XLA Ops:
  0.0 1.5 %copy-start.2 = (f32[2,1,2,1,256,256]{5,4,3,2,1,0:T(8,128)S(1)}, f32[2,1,2,1,256,256]{5,4,3,2,1,0:T(8,128)}, u32[]{:S(2)}) copy-start(f32[2,1,2,1,256,256]{5,4,3,2,1,0:T(8,128)} %param.5) | copy-start | bytes 3145732
  1.5 1.0 copy-start
  1.5 1.0 copy-start.1

commit v3 on v1

v3 whole, which is shorter than its diff:
```python
import jax
import jax.numpy as jnp
from jax import lax
from jax.experimental import pallas as pl
from jax.experimental.pallas import tpu as pltpu
from jax.sharding import PartitionSpec as P

FIRST = 8
DIAGS = 4
SIDE = 16
XS = 4
TOTAL = 32
MESH = pl.DeviceIdType.MESH


def arrived(ref, sem):
    pltpu.make_async_copy(ref, ref, sem).wait()


def wrap(x):
    return lax.rem(x + 2 * SIDE, SIDE)


def line_of(i):
    return lax.rem((i + FIRST) // XS + 2 * (i // SIDE), XS)


def dot(a, b):
    return jnp.dot(a, b, preferred_element_type=jnp.float32)


def halves(x):
    high = x.astype(jnp.bfloat16)
    return high, (x - high.astype(jnp.float32)).astype(jnp.bfloat16)


def left_dot(a, x):
    high, low = halves(x)
    return dot(a, high) + dot(a, low)


def right_dot(x, b):
    high, low = halves(x)
    return dot(high, b) + dot(low, b)


def kernel(
    schur, known, pairs, lam, out,
    row_f, row_s, col_f, col_s, vj, new_r, new_c, total, gap, fresh, solved,
    q_row_f, q_row_s, q_col_f, q_col_s, q_vj, q_new_r, q_new_c, q_out,
    s_src, s_ring_f, s_ring_s, s_chain_f, s_chain_s, s_chain_v, s_own, s_new, s_out,
):
    r = lax.axis_index("row")
    c = lax.axis_index("col")
    x_at, y_at = lax.rem(c, XS), c // XS
    e = wrap(c - r)
    later = []

    def remote(src, dst, send_sem, recv_sem, row, col):
        return pltpu.make_async_remote_copy(
            src_ref=src, dst_ref=dst, send_sem=send_sem, recv_sem=recv_sem,
            device_id=(row, col), device_id_type=MESH,
        )

    def run_if(cond, fn):
        pl.when(cond)(fn)

    def send(cond, *args):
        copy = remote(*args)
        run_if(cond, copy.start)
        later.append((cond, copy))

    def send_in_row(cond, src, dst, send_sem, recv_sem, col):
        run_if(cond & (col == c), pltpu.make_async_copy(src, dst, recv_sem).start)
        send(cond & (col != c), src, dst, send_sem, recv_sem, r, col)

    barrier = pltpu.get_barrier_semaphore()

    def meet(row, col):
        pl.semaphore_signal(barrier, inc=1, device_id=(row, col), device_id_type=MESH)

    def greet_line(step, carry):
        meet(lax.rem(r + step // XS, SIDE), XS * lax.rem(y_at + step, XS) + x_at)
        return carry

    def greet_row(step, carry):
        meet(r, XS * lax.rem(step, XS) + lax.rem(x_at + 1 + step // XS, XS))
        return carry

    lines = SIDE * XS - 1
    others = XS * (XS - 1)
    lax.fori_loop(1, lines + 1, greet_line, 0)
    lax.fori_loop(0, others, greet_row, 0)
    pl.semaphore_wait(barrier, lines + others)

    def seat(i):
        return wrap(i), XS * line_of(i) + x_at

    near = e < FIRST
    eb = jnp.minimum(e, FIRST - 1)
    places = []
    for t in (0, 1):
        k = r + SIDE * t
        j = k + e
        b = jnp.minimum(j // SIDE, 1)
        to_row = near & (k < TOTAL - FIRST)
        to_col = near & (j >= FIRST) & (j < TOTAL)
        last = jnp.minimum(DIAGS - 1, j - FIRST)
        i_to = jnp.maximum(j - FIRST - jnp.where(e >= DIAGS, 0, last), 0)
        places.append((b, to_row, to_col, seat(k)[1], seat(i_to)))
    for n, (ref, row_ref, col_ref, q_row, q_col) in enumerate(
        ((known, row_f, col_f, q_row_f, q_col_f), (schur, row_s, col_s, q_row_s, q_col_s))
    ):
        for t in (0, 1):
            b, to_row, to_col, col_to, entry = places[t]
            used = e >= n
            send_in_row(to_row & used, ref.at[t, b], row_ref.at[eb], s_src.at[t, 2 * n], q_row.at[eb], col_to)
            send(to_col & used, ref.at[t, b], col_ref.at[eb], s_src.at[t, 2 * n + 1], q_col.at[eb], *entry)

    mo = jnp.clip(e - FIRST, 0, DIAGS - 1)
    owner = (e >= FIRST) & (e < FIRST + DIAGS)
    owned = []
    for t in (0, 1):
        k = r + SIDE * t
        j = k + e
        b = jnp.minimum(j // SIDE, 1)
        slot = FIRST + mo
        owned.append(owner & (j < TOTAL))
        for d in range(DIAGS):
            fits = owner & (j + d < TOTAL) & (mo + d < DIAGS)
            col_to = XS * line_of(k) + lax.rem(x_at + d, XS)
            send_in_row(fits, schur.at[t, b], row_s.at[slot], s_own.at[t, 0, d], q_row_s.at[slot], col_to)
            if d:
                fits = owned[t] & (mo + d < DIAGS) & (k >= d)
                send(fits, schur.at[t, b], col_s.at[slot], s_own.at[t, 1, d], q_col_s.at[slot], *seat(jnp.maximum(k - d, 0)))

    for t in (0, 1):
        _, _, to_col, _, entry = places[t]
        send(to_col & (e == 0), pairs.at[t], vj, s_src.at[t, 4], q_vj.at[0], *entry)

    second = (r < TOTAL - SIDE - FIRST) & (y_at == r // XS)
    part = second | (y_at == line_of(r))
    t = jnp.where(second, 1, 0)
    i = r + SIDE * t
    m = lax.rem(x_at + SIDE - r, XS)
    j = i + FIRST + m
    real = part & (j < TOTAL)
    last = jnp.minimum(DIAGS - 1, i + m)
    up = real & (m < last)
    down = real & (m > 0)
    col_next = (XS * y_at + lax.rem(x_at + 1, XS), XS * y_at + lax.rem(x_at + XS - 1, XS))

    @pl.when(real)
    def _():
        rows = jnp.broadcast_to(lam[pl.ds(i, 1), :], total.shape).T
        gap[...] = 1.0 / (rows - lam[pl.ds(jnp.minimum(j, TOTAL - 1), 1), :])
        total[...] = jnp.zeros(total.shape, jnp.float32)

    kinds = (
        (row_f, q_row_f, s_ring_f, 0, col_f, s_chain_f, q_col_f),
        (row_s, q_row_s, s_ring_s, 1, col_s, s_chain_s, q_col_s),
    )

    def ring(kind, x, d):
        ref, sems, send_sems = kind[:3]
        return remote(ref.at[x], ref.at[x], send_sems.at[x, d], sems.at[x], r, col_next[d])

    def chain(kind, x, step):
        ref, send_sems, sems = kind[4:]
        return remote(ref.at[x], ref.at[x], send_sems.at[x], sems.at[x], *seat(jnp.maximum(i - step, 0)))

    def chain_v():
        return remote(vj, vj, s_chain_v.at[0], q_vj.at[0], *seat(i + 1))

    def row_entry(kind, start):
        ref, sems, least = kind[0], kind[1], kind[3]
        for x in (m, m + DIAGS):

            @pl.when(part & (x >= least))
            def _():
                if start:
                    arrived(ref.at[x], sems.at[x])
                    ring(kind, x, 0).start()
                    ring(kind, x, 1).start()
                else:
                    ring(kind, x, 0).wait_send()
                    ring(kind, x, 1).wait_send()

    def row_relay(kind, start):
        ref, sems, least = kind[0], kind[1], kind[3]
        base = lax.rem(m + (1 if least else DIAGS - 1), DIAGS)
        for x in (base, base + DIAGS):

            @pl.when(part & (x >= least))
            def _():
                if start:
                    arrived(ref.at[x], sems.at[x])
                    ring(kind, x, least).start()
                else:
                    ring(kind, x, least).wait_send()

    def col_relay(kind, depths, start):
        ref, _, sems = kind[4:]
        up_now, down_now = jnp.bool_(False), jnp.bool_(False)
        for depth in depths:
            up_now |= up & (m == depth)
            down_now |= down & (last - m == depth)

        def move(x, step):
            copy = chain(kind, x, step)
            if start:
                arrived(ref.at[x], sems.at[x])
                copy.start()
            else:
                copy.wait_send()

        def step(x, carry):
            run_if(up_now, lambda: move(x + DIAGS, 1))
            run_if(down_now & (x >= kind[3]), lambda: move(x, -1))
            return carry

        lax.fori_loop(0, DIAGS, step, 0)

    def first_hops(kind):
        row_entry(kind, True)
        col_relay(kind, (0,), True)
        col_relay(kind, (1,), True)

    def second_hops(kind):
        row_relay(kind, True)
        col_relay(kind, (2,), True)

    first_hops(kinds[0])
    first_hops(kinds[1])
    second_hops(kinds[0])
    second_hops(kinds[1])
    for depth in range(DIAGS - 1):

        @pl.when(down & (last - m == depth))
        def _():
            arrived(vj, q_vj.at[0])
            chain_v().start()

    def rest_f(x, carry):
        away = lax.rem(m - x + 2 * DIAGS, DIAGS)
        ends = jnp.where(x >= DIAGS, ~up, ~down)
        run_if(part & (away >= 2), lambda: arrived(row_f.at[x], q_row_f.at[x]))
        run_if(real & ends, lambda: arrived(col_f.at[x], q_col_f.at[x]))
        return carry

    lax.fori_loop(0, FIRST, rest_f, 0)

    def far(x, carry):
        @pl.when(real & (x < FIRST + m))
        def _():
            arrived(row_s.at[x], q_row_s.at[x])
            arrived(col_s.at[x], q_col_s.at[x])
            near_x = FIRST + m - x
            total[...] += dot(row_f[near_x], col_s[x]) - dot(row_s[x], col_f[near_x])

        @pl.when(real & (x == FIRST + m))
        def _():
            arrived(row_s.at[x], q_row_s.at[x])
            total[...] += dot(row_f[0], row_s[x]) - dot(row_s[x], col_f[0])

        return carry

    lax.fori_loop(FIRST, FIRST + DIAGS, far, 0)

    def rest_s(x, carry):
        away = lax.rem(m - x + 2 * DIAGS, DIAGS)
        ends = jnp.where(x >= DIAGS, ~up, ~down)
        run_if(part & ((away == 1) | (away == 2)), lambda: arrived(row_s.at[x], q_row_s.at[x]))
        run_if(real & ends, lambda: arrived(col_s.at[x], q_col_s.at[x]))

        @pl.when(real & (x > m))
        def _():
            near_x = FIRST + m - x
            total[...] += dot(row_f[near_x], col_s[x]) - dot(row_s[x], col_f[near_x])

        return carry

    lax.fori_loop(1, FIRST, rest_s, 0)
    run_if(real & ~down, lambda: arrived(vj, q_vj.at[0]))

    for before in range(DIAGS - 1):

        @pl.when(real & (m > before))
        def _():
            near_x = m - before
            arrived(new_r.at[before], q_new_r.at[before])
            arrived(new_c.at[before], q_new_c.at[before])
            total[...] += dot(new_r[before], col_s[near_x]) - dot(row_s[near_x], new_c[before])

    @pl.when(real)
    def _():
        x = left_dot(pairs[t, 1], total[...])
        x = right_dot(x, vj[0]) * gap[...]
        x = left_dot(pairs[t, 0], x)
        x = right_dot(x, vj[1])
        fresh[...] = x.astype(jnp.bfloat16)
        solved[...] = x

    mine = jnp.minimum(m, DIAGS - 2)
    for d in range(1, DIAGS):
        fits = real & (m + d < DIAGS)
        send(fits & (j + d < TOTAL), fresh, new_r.at[mine], s_new.at[0, d - 1], q_new_r.at[mine], r, XS * y_at + lax.rem(x_at + d, XS))
        send(fits & (i >= d), fresh, new_c.at[mine], s_new.at[1, d - 1], q_new_c.at[mine], *seat(jnp.maximum(i - d, 0)))
    send_in_row(real, solved, out.at[t], s_out.at[0], q_out.at[t], lax.rem(j, SIDE))

    for n in (0, 1):
        run_if(owned[n], lambda: arrived(out.at[n], q_out.at[n]))

    for cond, copy in later:
        run_if(cond, copy.wait_send)
    for kind in kinds:
        row_entry(kind, False)
        row_relay(kind, False)
        col_relay(kind, (0, 1, 2), False)
    run_if(down, lambda: chain_v().wait_send())


def exchange(schur, known, pairs, lam):
    bs = schur.shape[-1]
    half, full = jnp.bfloat16, jnp.float32
    dma = pltpu.SemaphoreType.DMA
    vmem = pl.BlockSpec(memory_space=pltpu.VMEM)
    return pl.pallas_call(
        kernel,
        out_shape=jax.ShapeDtypeStruct((2, bs, bs), full),
        in_specs=[vmem] * 4,
        out_specs=vmem,
        scratch_shapes=[
            pltpu.VMEM((FIRST, bs, bs), half),
            pltpu.VMEM((FIRST + DIAGS, bs, bs), half),
            pltpu.VMEM((FIRST, bs, bs), half),
            pltpu.VMEM((FIRST + DIAGS, bs, bs), half),
            pltpu.VMEM((2, bs, bs), half),
            pltpu.VMEM((DIAGS - 1, bs, bs), half),
            pltpu.VMEM((DIAGS - 1, bs, bs), half),
            pltpu.VMEM((bs, bs), full),
            pltpu.VMEM((bs, bs), full),
            pltpu.VMEM((bs, bs), half),
            pltpu.VMEM((bs, bs), full),
            dma((FIRST,)), dma((FIRST + DIAGS,)), dma((FIRST,)), dma((FIRST + DIAGS,)),
            dma((1,)), dma((DIAGS - 1,)), dma((DIAGS - 1,)), dma((2,)),
            dma((2, 5)), dma((FIRST, 2)), dma((FIRST, 2)), dma((FIRST,)), dma((FIRST,)),
            dma((1,)), dma((2, 2, DIAGS)), dma((2, DIAGS - 1)), dma((1,)),
        ],
        compiler_params=pltpu.CompilerParams(
            collective_id=0, has_side_effects=True, vmem_limit_bytes=40 * 1024 * 1024
        ),
    )(schur, known, pairs, lam)


def body(schur_blocks, known_blocks, eigen_pairs, eigenvalues):
    known = known_blocks[:, 0, :, 0]
    solved = exchange(
        schur_blocks[:, 0, :, 0],
        known.astype(jnp.bfloat16),
        eigen_pairs[:, 0].astype(jnp.bfloat16),
        eigenvalues,
    )
    rows = lax.axis_index("row") + SIDE * jnp.arange(2)[:, None]
    cols = lax.axis_index("col") + SIDE * jnp.arange(2)[None, :]
    away = cols - rows
    new = (away >= FIRST) & (away < FIRST + DIAGS)
    output = jnp.where(new[:, :, None, None], solved[:, None], known)
    return output[:, None, :, None]


def solution(mesh):
    return jax.shard_map(
        body,
        mesh=mesh,
        in_specs=(
            P(None, "row", None, "col", None, None),
            P(None, "row", None, "col", None, None),
            P(None, "row", None, None, None),
            P(),
        ),
        out_specs=P(None, "row", None, "col", None, None),
        check_vma=False,
    )
```

time: 307 us -> 97.4 us (0.32)
  the two profiles are of different devices: /device:TPU:22 before, /device:TPU:1 now
where the time goes in v3:
time: 97.4 us; the launch traced here: 97.3 us
  Pallas kernels  93.6 us (96%)
  other arithmetic  2.62 us (3%)
  local copies, waits for them, and re-layouts  1.09 us (1%)
    pallas_call x1, Pallas kernels, exchange(): pl.pallas_call(kernel, out_shape=jax.ShapeDtypeStruct((2, bs, bs), full),...  93.6 us

profile of v3, /device:TPU:1, one launch (start us, length us, event | category | flops | bytes accessed | tf_op | source)
XLA Modules:
  0.0 97.3 jit_solution(17353123625668547295)
XLA Ops:
  0.0 0.0 copy-start.2
  0.0 0.1 compare_and_fusion
  0.1 1.4 %fusion.1.pairs = bf16[2,2,256,256]{3,2,1,0:T(8,128)(2,1)S(1)} fusion(f32[2,1,2,256,256]{4,3,2,1,0:T(8,128)} %param.6), kind=kLoop, calls=%fused_computation.3 | loop fusion | flops 262144 | bytes 1572864 | tf_op jit(solution)/shard_map/convert_element_type | solution.py:361
  1.4 0.1 copy-done.2
  1.5 0.0 copy-start
  1.5 0.0 copy-start.1
  1.5 0.1 fusion.known
  1.6 1.0 %copy-done = bf16[2,1,2,1,256,256]{5,4,3,2,1,0:T(8,128)(2,1)S(1)} copy-done((bf16[2,1,2,1,256,256]{5,4,3,2,1,0:T(8,128)(2,1)S(1)}, bf16[2,1,2,1,256,256]{5,4,3,2,1,0:T(8,128)(2,1)}, u32[]{:S(2)}) %copy-start) | copy-done | bytes 524312
  2.6 0.0 copy-done.1
  2.6 93.6 %shard_map.46 = f32[2,256,256]{2,1,0:T(8,128)S(1)} custom-call(bf16[2,2,256,256]{3,2,1,0:T(8,128)(2,1)S(1)} %bitcast.13, bf16[2,2,256,256]{3,2,1,0:T(8,128)(2,1)S(1)} %fusion.known, bf16[2,2,256,256]{3,2,1,0:T(8,128)(2,1)S(1)} %fusion.1.pairs, f32[32,256]{1,0:T(8,128)S(1)} %copy-done.1), custom_call_target="tpu_custom_call" | custom-call | tf_op jit(solution)/shard_map/pallas_call | solution.py:328
  96.2 1.1 %broadcast_select_fusion = f32[2,1,2,1,256,256]{5,4,3,2,1,0:T(8,128)} fusion(f32[2,1,2,1,256,256]{5,4,3,2,1,0:T(8,128)S(1)} %copy-done.2, f32[2,256,256]{2,1,0:T(8,128)S(1)} %shard_map.46, pred[2,2]{1,0:T(4,128)(4,1)S(1)} %compare_and_fusion), kind=kLoop, calls=%fused_computation.4 | loop fusion | flops 262144 | bytes 2621444 | tf_op jit(solution)/shard_map/jit(_where)/select_n | solution.py:368
  (1 shorter events, 0.0 us)
Async XLA Ops:
  0.0 1.5 %copy-start.2 = (f32[2,1,2,1,256,256]{5,4,3,2,1,0:T(8,128)S(1)}, f32[2,1,2,1,256,256]{5,4,3,2,1,0:T(8,128)}, u32[]{:S(2)}) copy-start(f32[2,1,2,1,256,256]{5,4,3,2,1,0:T(8,128)} %param.5) | copy-start | bytes 3145732
  1.5 1.0 %copy-start = (bf16[2,1,2,1,256,256]{5,4,3,2,1,0:T(8,128)(2,1)S(1)}, bf16[2,1,2,1,256,256]{5,4,3,2,1,0:T(8,128)(2,1)}, u32[]{:S(2)}) copy-start(bf16[2,1,2,1,256,256]{5,4,3,2,1,0:T(8,128)(2,1)} %param.4) | copy-start | bytes 1572868
  1.5 1.0 %copy-start.1 = (f32[32,256]{1,0:T(8,128)S(1)}, f32[32,256]{1,0:T(8,128)}, u32[]{:S(2)}) copy-start(f32[32,256]{1,0:T(8,128)} %lam.1) | copy-start | bytes 98308

commit v4 on v3

--- a/solution.py
+++ b/solution.py
@@ -12,6 +12,10 @@
 TOTAL = 32
 MESH = pl.DeviceIdType.MESH
 
+SENDS = ("cF0", "cF1", "rF1", "rS0", "rF0", "rS1", "cS0", "cS1", "own", "v")
+WAITS = ("eF", "0F", "1F", "eS", "0S", "lS", "2F", "1S", "lF", "v0", "v1", "2S", "v2")
+TURN = {"F": 1, "S": 1}
+
 
 def arrived(ref, sem):
     pltpu.make_async_copy(ref, ref, sem).wait()
@@ -22,7 +26,7 @@
 
 
 def line_of(i):
-    return lax.rem((i + FIRST) // XS + 2 * (i // SIDE), XS)
+    return lax.rem((i + FIRST) // XS + i // SIDE, XS)
 
 
 def dot(a, b):
@@ -108,24 +112,27 @@
         last = jnp.minimum(DIAGS - 1, j - FIRST)
         i_to = jnp.maximum(j - FIRST - jnp.where(e >= DIAGS, 0, last), 0)
         places.append((b, to_row, to_col, seat(k)[1], seat(i_to)))
-    for n, (ref, row_ref, col_ref, q_row, q_col) in enumerate(
-        ((known, row_f, col_f, q_row_f, q_col_f), (schur, row_s, col_s, q_row_s, q_col_s))
-    ):
-        for t in (0, 1):
-            b, to_row, to_col, col_to, entry = places[t]
-            used = e >= n
-            send_in_row(to_row & used, ref.at[t, b], row_ref.at[eb], s_src.at[t, 2 * n], q_row.at[eb], col_to)
-            send(to_col & used, ref.at[t, b], col_ref.at[eb], s_src.at[t, 2 * n + 1], q_col.at[eb], *entry)
+    def send_near(group, kind, t):
+        n = "FS".index(kind)
+        b, to_row, to_col, col_to, entry = places[t]
+        ref = (known, schur)[n]
+        used = e >= n
+        if group == "r":
+            dst, sems = ((row_f, q_row_f), (row_s, q_row_s))[n]
+            send_in_row(to_row & used, ref.at[t, b], dst.at[eb], s_src.at[t, 2 * n], sems.at[eb], col_to)
+        else:
+            dst, sems = ((col_f, q_col_f), (col_s, q_col_s))[n]
+            send(to_col & used, ref.at[t, b], dst.at[eb], s_src.at[t, 2 * n + 1], sems.at[eb], *entry)
 
     mo = jnp.clip(e - FIRST, 0, DIAGS - 1)
     owner = (e >= FIRST) & (e < FIRST + DIAGS)
-    owned = []
-    for t in (0, 1):
+    owned = [owner & (r + SIDE * t + e < TOTAL) for t in (0, 1)]
+
+    def send_own(t):
         k = r + SIDE * t
         j = k + e
         b = jnp.minimum(j // SIDE, 1)
         slot = FIRST + mo
-        owned.append(owner & (j < TOTAL))
         for d in range(DIAGS):
             fits = owner & (j + d < TOTAL) & (mo + d < DIAGS)
             col_to = XS * line_of(k) + lax.rem(x_at + d, XS)
@@ -134,11 +141,18 @@
                 fits = owned[t] & (mo + d < DIAGS) & (k >= d)
                 send(fits, schur.at[t, b], col_s.at[slot], s_own.at[t, 1, d], q_col_s.at[slot], *seat(jnp.maximum(k - d, 0)))
 
-    for t in (0, 1):
-        _, _, to_col, _, entry = places[t]
-        send(to_col & (e == 0), pairs.at[t], vj, s_src.at[t, 4], q_vj.at[0], *entry)
-
-    second = (r < TOTAL - SIDE - FIRST) & (y_at == r // XS)
+    for token in SENDS:
+        if token == "own":
+            send_own(0)
+            send_own(1)
+        elif token == "v":
+            for t in (0, 1):
+                _, _, to_col, _, entry = places[t]
+                send(to_col & (e == 0), pairs.at[t], vj, s_src.at[t, 4], q_vj.at[0], *entry)
+        else:
+            send_near(token[0], token[1], int(token[2]))
+
+    second = (r < TOTAL - SIDE - FIRST) & (y_at == line_of(r + SIDE))
     part = second | (y_at == line_of(r))
     t = jnp.where(second, 1, 0)
     i = r + SIDE * t
@@ -188,16 +202,18 @@
 
     def row_relay(kind, start):
         ref, sems, least = kind[0], kind[1], kind[3]
-        base = lax.rem(m + (1 if least else DIAGS - 1), DIAGS)
+        turn = TURN["FS"[least]]
+        base = lax.rem(m + DIAGS - turn, DIAGS)
         for x in (base, base + DIAGS):
 
             @pl.when(part & (x >= least))
             def _():
+                copy = ring(kind, x, 0 if turn == 1 else 1)
                 if start:
                     arrived(ref.at[x], sems.at[x])
-                    ring(kind, x, least).start()
+                    copy.start()
                 else:
-                    ring(kind, x, least).wait_send()
+                    copy.wait_send()
 
     def col_relay(kind, depths, start):
         ref, _, sems = kind[4:]
@@ -221,30 +237,32 @@
 
         lax.fori_loop(0, DIAGS, step, 0)
 
-    def first_hops(kind):
-        row_entry(kind, True)
-        col_relay(kind, (0,), True)
-        col_relay(kind, (1,), True)
-
-    def second_hops(kind):
-        row_relay(kind, True)
-        col_relay(kind, (2,), True)
-
-    first_hops(kinds[0])
-    first_hops(kinds[1])
-    second_hops(kinds[0])
-    second_hops(kinds[1])
-    for depth in range(DIAGS - 1):
-
-        @pl.when(down & (last - m == depth))
-        def _():
-            arrived(vj, q_vj.at[0])
-            chain_v().start()
+    for token in WAITS:
+        if token[0] == "v":
+            depth = int(token[1])
+
+            @pl.when(down & (last - m == depth))
+            def _():
+                arrived(vj, q_vj.at[0])
+                chain_v().start()
+
+        else:
+            kind = kinds["FS".index(token[1])]
+            if token[0] == "e":
+                row_entry(kind, True)
+            elif token[0] == "l":
+                row_relay(kind, True)
+            else:
+                col_relay(kind, (int(token[0]),), True)
+
+    def kept(kind, x):
+        away = lax.rem(m - x + 2 * DIAGS, DIAGS)
+        relay = 1 if TURN[kind] == 1 else DIAGS - 1
+        return part & (away != 0) & (away != relay)
 
     def rest_f(x, carry):
-        away = lax.rem(m - x + 2 * DIAGS, DIAGS)
         ends = jnp.where(x >= DIAGS, ~up, ~down)
-        run_if(part & (away >= 2), lambda: arrived(row_f.at[x], q_row_f.at[x]))
+        run_if(kept("F", x), lambda: arrived(row_f.at[x], q_row_f.at[x]))
         run_if(real & ends, lambda: arrived(col_f.at[x], q_col_f.at[x]))
         return carry
 
@@ -268,9 +286,8 @@
     lax.fori_loop(FIRST, FIRST + DIAGS, far, 0)
 
     def rest_s(x, carry):
-        away = lax.rem(m - x + 2 * DIAGS, DIAGS)
         ends = jnp.where(x >= DIAGS, ~up, ~down)
-        run_if(part & ((away == 1) | (away == 2)), lambda: arrived(row_s.at[x], q_row_s.at[x]))
+        run_if(kept("S", x), lambda: arrived(row_s.at[x], q_row_s.at[x]))
         run_if(real & ends, lambda: arrived(col_s.at[x], q_col_s.at[x]))
 
         @pl.when(real & (x > m))

time: 97.4 us -> 85.4 us (0.88)
  the two profiles are of different devices: /device:TPU:1 before, /device:TPU:94 now
where the time goes in v4:
time: 85.4 us; the launch traced here: 85.3 us
  Pallas kernels  81.5 us (95%)
  other arithmetic  2.62 us (3%)
  local copies, waits for them, and re-layouts  1.09 us (1%)
    pallas_call x1, Pallas kernels, exchange(): pl.pallas_call(kernel, out_shape=jax.ShapeDtypeStruct((2, bs, bs), full),...  81.5 us

profile of v4, /device:TPU:94, one launch (start us, length us, event | category | flops | bytes accessed | tf_op | source)
XLA Modules:
  0.0 85.3 jit_solution(6158922218770209983)
XLA Ops:
  0.0 0.0 copy-start.2
  0.0 0.1 compare_and_fusion
  0.1 1.4 %fusion.1.pairs = bf16[2,2,256,256]{3,2,1,0:T(8,128)(2,1)S(1)} fusion(f32[2,1,2,256,256]{4,3,2,1,0:T(8,128)} %param.6), kind=kLoop, calls=%fused_computation.3 | loop fusion | flops 262144 | bytes 1572864 | tf_op jit(solution)/shard_map/convert_element_type | solution.py:378
  1.4 0.1 copy-done.2
  1.5 0.0 copy-start
  1.5 0.0 copy-start.1
  1.5 0.1 fusion.known
  1.6 1.0 %copy-done = bf16[2,1,2,1,256,256]{5,4,3,2,1,0:T(8,128)(2,1)S(1)} copy-done((bf16[2,1,2,1,256,256]{5,4,3,2,1,0:T(8,128)(2,1)S(1)}, bf16[2,1,2,1,256,256]{5,4,3,2,1,0:T(8,128)(2,1)}, u32[]{:S(2)}) %copy-start) | copy-done | bytes 524312
  2.6 0.0 copy-done.1
  2.6 81.5 %shard_map.46 = f32[2,256,256]{2,1,0:T(8,128)S(1)} custom-call(bf16[2,2,256,256]{3,2,1,0:T(8,128)(2,1)S(1)} %bitcast.13, bf16[2,2,256,256]{3,2,1,0:T(8,128)(2,1)S(1)} %fusion.known, bf16[2,2,256,256]{3,2,1,0:T(8,128)(2,1)S(1)} %fusion.1.pairs, f32[32,256]{1,0:T(8,128)S(1)} %copy-done.1), custom_call_target="tpu_custom_call" | custom-call | tf_op jit(solution)/shard_map/pallas_call | solution.py:345
  84.1 1.1 %broadcast_select_fusion = f32[2,1,2,1,256,256]{5,4,3,2,1,0:T(8,128)} fusion(f32[2,1,2,1,256,256]{5,4,3,2,1,0:T(8,128)S(1)} %copy-done.2, f32[2,256,256]{2,1,0:T(8,128)S(1)} %shard_map.46, pred[2,2]{1,0:T(4,128)(4,1)S(1)} %compare_and_fusion), kind=kLoop, calls=%fused_computation.4 | loop fusion | flops 262144 | bytes 2621444 | tf_op jit(solution)/shard_map/jit(_where)/select_n | solution.py:385
  (1 shorter events, 0.0 us)
Async XLA Ops:
  0.0 1.5 %copy-start.2 = (f32[2,1,2,1,256,256]{5,4,3,2,1,0:T(8,128)S(1)}, f32[2,1,2,1,256,256]{5,4,3,2,1,0:T(8,128)}, u32[]{:S(2)}) copy-start(f32[2,1,2,1,256,256]{5,4,3,2,1,0:T(8,128)} %param.5) | copy-start | bytes 3145732
  1.5 1.0 %copy-start = (bf16[2,1,2,1,256,256]{5,4,3,2,1,0:T(8,128)(2,1)S(1)}, bf16[2,1,2,1,256,256]{5,4,3,2,1,0:T(8,128)(2,1)}, u32[]{:S(2)}) copy-start(bf16[2,1,2,1,256,256]{5,4,3,2,1,0:T(8,128)(2,1)} %param.4) | copy-start | bytes 1572868
  1.5 1.0 %copy-start.1 = (f32[32,256]{1,0:T(8,128)S(1)}, f32[32,256]{1,0:T(8,128)}, u32[]{:S(2)}) copy-start(f32[32,256]{1,0:T(8,128)} %lam.1) | copy-start | bytes 98308

commit v5 on v4

v5 whole, which is shorter than its diff:
```python
import jax
import jax.numpy as jnp
from jax import lax
from jax.experimental import pallas as pl
from jax.experimental.pallas import tpu as pltpu
from jax.sharding import PartitionSpec as P

FIRST = 8
DIAGS = 4
SIDE = 16
XS = 4
TOTAL = 32
AWAY = 4
MESH = pl.DeviceIdType.MESH

SENDS = ("cF0", "cS0", "cF1", "cS1", "rF0", "rS0", "rF1", "rS1", "own", "x", "v")
WAITS = (("0", "e", "1", "l", "2", "v0", "v1", "v2"), ("0", "e", "1", "l", "2", "3"))
ENTRY = ((3, 3, 3, 3, 0, 0, 0, 0), (0, 0, 0, 0, 0, 1, 2, 3))
TURN = ((1, 1), (1, 1))
CHAIN_ORDER = (4, 0, 5, 1, 6, 2, 7, 3)


def arrived(ref, sem):
    pltpu.make_async_copy(ref, ref, sem).wait()


def wrap(x):
    return lax.rem(x + 2 * SIDE, SIDE)


def line_of(i, second):
    return lax.rem((i + FIRST) // XS + (1 + 2 * second) * (i // SIDE), XS)


def pick(index, table):
    chosen = jnp.int32(table[0])
    for n, value in enumerate(table[1:], 1):
        chosen = jnp.where(index == n, value, chosen)
    return chosen


def dot(a, b):
    return jnp.dot(a, b, preferred_element_type=jnp.float32)


def halves(x):
    high = x.astype(jnp.bfloat16)
    return high, (x - high.astype(jnp.float32)).astype(jnp.bfloat16)


def left_dot(a, x):
    high, low = halves(x)
    return dot(a, high) + dot(a, low)


def right_dot(x, b):
    high, low = halves(x)
    return dot(high, b) + dot(low, b)


def kernel(
    schur, known, pairs, lam, out,
    ring, chain, near_s, vj, new_r, new_c, other, total, gap, fresh, solved,
    q_ring, q_chain, q_near, q_vj, q_new_r, q_new_c, q_other, q_out,
    s_src, s_ring, s_chain, s_v, s_own, s_near, s_new, s_out,
):
    r = lax.axis_index("row")
    c = lax.axis_index("col")
    x_at, y_at = lax.rem(c, XS), c // XS
    e = wrap(c - r)
    later = []

    def remote(src, dst, send_sem, recv_sem, row, col):
        return pltpu.make_async_remote_copy(
            src_ref=src, dst_ref=dst, send_sem=send_sem, recv_sem=recv_sem,
            device_id=(row, col), device_id_type=MESH,
        )

    def run_if(cond, fn):
        pl.when(cond)(fn)

    def send(cond, src, dst, send_sem, recv_sem, row, col):
        copy = remote(src, dst, send_sem, recv_sem, row, col)
        run_if(cond, copy.start)
        later.append((cond, copy))

    def send_any(cond, src, dst, send_sem, recv_sem, row, col):
        here = (row == r) & (col == c)
        run_if(cond & here, pltpu.make_async_copy(src, dst, recv_sem).start)
        send(cond & ~here, src, dst, send_sem, recv_sem, row, col)

    def seat(i, second, x=x_at):
        return wrap(i + AWAY * second), XS * line_of(i, second) + x

    barrier = pltpu.get_barrier_semaphore()

    def meet(row, col):
        pl.semaphore_signal(barrier, inc=1, device_id=(row, col), device_id_type=MESH)

    def greet_line(step, carry):
        meet(lax.rem(r + step // XS, SIDE), XS * lax.rem(y_at + step, XS) + x_at)
        return carry

    def greet_row(step, carry):
        col = XS * lax.rem(step, XS) + lax.rem(x_at + 1 + step // XS, XS)
        meet(r, col)
        meet(wrap(r + AWAY), col)
        meet(wrap(r - AWAY), col)
        return carry

    lines = SIDE * XS - 1
    others = XS * (XS - 1)
    lax.fori_loop(1, lines + 1, greet_line, 0)
    lax.fori_loop(0, others, greet_row, 0)
    pl.semaphore_wait(barrier, lines + 3 * others)

    near = e < FIRST
    eb = jnp.minimum(e, FIRST - 1)
    places = []
    for t in (0, 1):
        k = r + SIDE * t
        j = k + e
        b = jnp.minimum(j // SIDE, 1)
        last = jnp.clip(j - FIRST, 0, DIAGS - 1)
        to_ring = near & (k < TOTAL - FIRST)
        to_chain = near & (j >= FIRST) & (j < TOTAL)
        entries = [
            seat(jnp.maximum(j - FIRST - jnp.minimum(pick(eb, ENTRY[n]), last), 0), n) for n in (0, 1)
        ]
        v_entry = seat(jnp.maximum(j - FIRST - last, 0), 0)
        places.append((k, j, b, to_ring, to_chain, entries, v_entry))

    mo = jnp.clip(e - FIRST, 0, DIAGS - 1)
    owner = (e >= FIRST) & (e < FIRST + DIAGS)
    owned = [owner & (places[t][1] < TOTAL) for t in (0, 1)]

    def send_near(group, kind, t):
        k, j, b, to_ring, to_chain, entries, _ = places[t]
        n = "FS".index(kind)
        src = (known, schur)[n].at[t, b]
        used = e >= n
        at = 2 * n + (group == "c")
        if group == "r":
            send_any(to_ring & used, src, ring.at[eb], s_src.at[t, at], q_ring.at[eb], *seat(k, n))
        else:
            send_any(to_chain & used, src, chain.at[eb], s_src.at[t, at], q_chain.at[eb], *entries[1 - n])

    def send_own(t):
        k, j, b = places[t][:3]
        slot = FIRST + mo
        for d in range(DIAGS):
            fits = owner & (j + d < TOTAL) & (mo + d < DIAGS)
            send(fits, schur.at[t, b], ring.at[slot], s_own.at[t, 0, d], q_ring.at[slot], *seat(k, 1, lax.rem(x_at + d, XS)))
            fits = owned[t] & (mo + d < DIAGS) & (k >= d)
            send_any(fits, schur.at[t, b], chain.at[slot], s_own.at[t, 1, d], q_chain.at[slot], *seat(jnp.maximum(k - d, 0), 0))

    def send_close(t):
        k, j, b = places[t][:3]
        slot = jnp.clip(e - 1, 0, DIAGS - 2)
        for d in range(DIAGS - 1):
            fits = (e >= 1) & (e + d < DIAGS) & (j + FIRST + d < TOTAL)
            send_any(fits, schur.at[t, b], near_s.at[slot], s_near.at[t, d], q_near.at[slot], *seat(k, 0, lax.rem(x_at + d, XS)))

    for token in SENDS:
        if token == "own":
            send_own(0)
            send_own(1)
        elif token == "x":
            send_close(0)
            send_close(1)
        elif token == "v":
            for t in (0, 1):
                send(places[t][4] & (e == 0), pairs.at[t], vj, s_src.at[t, 4], q_vj.at[0], *places[t][6])
        else:
            send_near(token[0], token[1], int(token[2]))

    i0 = wrap(r - AWAY)
    few = TOTAL - SIDE - FIRST
    first0, first1 = y_at == line_of(r, 0), (r < few) & (y_at == line_of(r + SIDE, 0))
    second0, second1 = y_at == line_of(i0, 1), (i0 < few) & (y_at == line_of(i0 + SIDE, 1))
    is_second = second0 | second1
    part = first0 | first1 | is_second
    kind = jnp.where(is_second, 1, 0)
    t = jnp.where(first1 | second1, 1, 0)
    i = jnp.where(is_second, i0, r) + SIDE * t
    m = lax.rem(x_at + 2 * SIDE - i, XS)
    j = i + FIRST + m
    real = part & (j < TOTAL)
    last = jnp.minimum(DIAGS - 1, i + m)
    takes = (part & ~is_second, is_second)
    adds = (real & ~is_second, real & is_second)
    col_next = (XS * y_at + lax.rem(x_at + 1, XS), XS * y_at + lax.rem(x_at + XS - 1, XS))

    @pl.when(adds[0])
    def _():
        rows = jnp.broadcast_to(lam[pl.ds(i, 1), :], total.shape).T
        gap[...] = 1.0 / (rows - lam[pl.ds(jnp.minimum(j, TOTAL - 1), 1), :])

    @pl.when(real)
    def _():
        total[...] = jnp.zeros(total.shape, jnp.float32)

    def member(step):
        return seat(jnp.maximum(i - step, 0), kind)

    def ring_copy(x, d):
        return remote(ring.at[x], ring.at[x], s_ring.at[x, d], q_ring.at[x], r, col_next[d])

    def chain_copy(x, d):
        return remote(chain.at[x], chain.at[x], s_chain.at[x, d], q_chain.at[x], *member(1 - 2 * d))

    def v_copy():
        return remote(vj, vj, s_v.at[0], q_vj.at[0], *member(-1))

    def ring_first(n, start):
        for x in (m, m + DIAGS):

            @pl.when(takes[n] & (x >= n))
            def _():
                if start:
                    arrived(ring.at[x], q_ring.at[x])
                for d in (0, 1):
                    ring_copy(x, d).start() if start else ring_copy(x, d).wait_send()

    def ring_second(n, start):
        for high in (0, 1):
            turn = TURN[n][high]
            x = lax.rem(m + DIAGS - turn, DIAGS) + DIAGS * high

            @pl.when(takes[n] & (x >= n))
            def _():
                copy = ring_copy(x, 0 if turn == 1 else 1)
                if start:
                    arrived(ring.at[x], q_ring.at[x])
                    copy.start()
                else:
                    copy.wait_send()

    def chain_moves(n, x):
        at = jnp.minimum(ENTRY[n][x], last)
        up = adds[n] & (m >= at) & (m < last)
        down = adds[n] & (m <= at) & (m > 0)
        return up, down, jnp.abs(m - at)

    def chain_slots(n):
        return [x for x in CHAIN_ORDER if x + n > 0]

    def chain_hop(n, depth):
        for x in chain_slots(n):
            up, down, hops = chain_moves(n, x)
            now = hops == depth
            run_if((up | down) & now, lambda: arrived(chain.at[x], q_chain.at[x]))
            run_if(up & now, chain_copy(x, 0).start)
            run_if(down & now, chain_copy(x, 1).start)

    v_moves = adds[0] & (m > 0)

    def v_hop(depth):
        @pl.when(v_moves & (last - m == depth))
        def _():
            arrived(vj, q_vj.at[0])
            v_copy().start()

    for n in (0, 1):
        for token in WAITS[n]:
            if token == "e":
                ring_first(n, True)
            elif token == "l":
                ring_second(n, True)
            elif token[0] == "v":
                v_hop(int(token[1]))
            else:
                chain_hop(n, int(token))

    def ring_rest(n, x):
        away = lax.rem(m - x + 2 * DIAGS, DIAGS)
        turn = TURN[n][x // DIAGS]
        mine = takes[n] & (away != 0) & (away != lax.rem(turn + DIAGS, DIAGS))
        run_if(mine, lambda: arrived(ring.at[x], q_ring.at[x]))

    def chain_rest(n, x):
        up, down, _ = chain_moves(n, x)
        run_if(adds[n] & ~(up | down), lambda: arrived(chain.at[x], q_chain.at[x]))

    def accumulate(x):
        other_x = FIRST + m - x
        total[...] += dot(ring[jnp.where(is_second, x, other_x)], chain[jnp.where(is_second, other_x, x)])

    for x in range(FIRST):
        ring_rest(0, x)
        chain_rest(1, x)

    def far(x, carry):
        @pl.when(real & (x <= FIRST + m))
        def _():
            run_if(~is_second, lambda: arrived(chain.at[x], q_chain.at[x]))
            run_if(is_second, lambda: arrived(ring.at[x], q_ring.at[x]))
            accumulate(x)

        return carry

    lax.fori_loop(FIRST, FIRST + DIAGS, far, 0)
    for x in range(1, FIRST):
        chain_rest(0, x)
        ring_rest(1, x)
        run_if(real & (x > m), lambda: accumulate(x))

    @pl.when(adds[1])
    def _():
        fresh[...] = total[...].astype(jnp.bfloat16)

    send(adds[1], fresh, other, s_out.at[1], q_other.at[0], *seat(i, 0))

    @pl.when(adds[0])
    def _():
        arrived(other, q_other.at[0])
        total[...] -= other[...].astype(jnp.float32)

    run_if(adds[0] & (m == 0), lambda: arrived(vj, q_vj.at[0]))

    for before in range(DIAGS - 1):

        @pl.when(adds[0] & (m > before))
        def _():
            arrived(near_s.at[before], q_near.at[before])

    for before in range(DIAGS - 1):

        @pl.when(adds[0] & (m > before))
        def _():
            away = m - before
            arrived(new_r.at[before], q_new_r.at[before])
            arrived(new_c.at[before], q_new_c.at[before])
            total[...] += dot(new_r[before], chain[away]) - dot(near_s[away - 1], new_c[before])

    @pl.when(adds[0])
    def _():
        x = left_dot(pairs[t, 1], total[...])
        x = right_dot(x, vj[0]) * gap[...]
        x = left_dot(pairs[t, 0], x)
        x = right_dot(x, vj[1])
        fresh[...] = x.astype(jnp.bfloat16)
        solved[...] = x

    mine = jnp.minimum(m, DIAGS - 2)
    for d in range(1, DIAGS):
        fits = adds[0] & (m + d < DIAGS)
        send(fits & (j + d < TOTAL), fresh, new_r.at[mine], s_new.at[0, d - 1], q_new_r.at[mine], r, XS * y_at + lax.rem(x_at + d, XS))
        send(fits & (i >= d), fresh, new_c.at[mine], s_new.at[1, d - 1], q_new_c.at[mine], *seat(jnp.maximum(i - d, 0), 0))
    send_any(adds[0], solved, out.at[t], s_out.at[0], q_out.at[t], wrap(i), lax.rem(j, SIDE))

    for n in (0, 1):
        run_if(owned[n], lambda: arrived(out.at[n], q_out.at[n]))

    for cond, copy in later:
        run_if(cond, copy.wait_send)
    for n in (0, 1):
        ring_first(n, False)
        ring_second(n, False)
        for x in chain_slots(n):
            up, down, _ = chain_moves(n, x)
            run_if(up, chain_copy(x, 0).wait_send)
            run_if(down, chain_copy(x, 1).wait_send)
    run_if(v_moves, lambda: v_copy().wait_send())


def exchange(schur, known, pairs, lam):
    bs = schur.shape[-1]
    half, full = jnp.bfloat16, jnp.float32
    dma = pltpu.SemaphoreType.DMA
    vmem = pl.BlockSpec(memory_space=pltpu.VMEM)
    band = FIRST + DIAGS
    return pl.pallas_call(
        kernel,
        out_shape=jax.ShapeDtypeStruct((2, bs, bs), full),
        in_specs=[vmem] * 4,
        out_specs=vmem,
        scratch_shapes=[
            pltpu.VMEM((band, bs, bs), half),
            pltpu.VMEM((band, bs, bs), half),
            pltpu.VMEM((DIAGS - 1, bs, bs), half),
            pltpu.VMEM((2, bs, bs), half),
            pltpu.VMEM((DIAGS - 1, bs, bs), half),
            pltpu.VMEM((DIAGS - 1, bs, bs), half),
            pltpu.VMEM((bs, bs), half),
            pltpu.VMEM((bs, bs), full),
            pltpu.VMEM((bs, bs), full),
            pltpu.VMEM((bs, bs), half),
            pltpu.VMEM((bs, bs), full),
            dma((band,)), dma((band,)), dma((DIAGS - 1,)), dma((1,)),
            dma((DIAGS - 1,)), dma((DIAGS - 1,)), dma((1,)), dma((2,)),
            dma((2, 5)), dma((band, 2)), dma((band, 2)), dma((1,)), dma((2, 2, DIAGS)),
            dma((2, DIAGS - 1)), dma((2, DIAGS - 1)), dma((2,)),
        ],
        compiler_params=pltpu.CompilerParams(
            collective_id=0, has_side_effects=True, vmem_limit_bytes=40 * 1024 * 1024
        ),
    )(schur, known, pairs, lam)


def body(schur_blocks, known_blocks, eigen_pairs, eigenvalues):
    known = known_blocks[:, 0, :, 0]
    solved = exchange(
        schur_blocks[:, 0, :, 0],
        known.astype(jnp.bfloat16),
        eigen_pairs[:, 0].astype(jnp.bfloat16),
        eigenvalues,
    )
    rows = lax.axis_index("row") + SIDE * jnp.arange(2)[:, None]
    cols = lax.axis_index("col") + SIDE * jnp.arange(2)[None, :]
    away = cols - rows
    new = (away >= FIRST) & (away < FIRST + DIAGS)
    output = jnp.where(new[:, :, None, None], solved[:, None], known)
    return output[:, None, :, None]


def solution(mesh):
    return jax.shard_map(
        body,
        mesh=mesh,
        in_specs=(
            P(None, "row", None, "col", None, None),
            P(None, "row", None, "col", None, None),
            P(None, "row", None, None, None),
            P(),
        ),
        out_specs=P(None, "row", None, "col", None, None),
        check_vma=False,
    )
```

time: 85.4 us -> 83.7 us (0.980)
  the two profiles are of different devices: /device:TPU:94 before, /device:TPU:22 now
where the time goes in v5:
time: 83.7 us; the launch traced here: 83.5 us
  Pallas kernels  79.8 us (95%)
  other arithmetic  2.62 us (3%)
  local copies, waits for them, and re-layouts  1.09 us (1%)
    pallas_call x1, Pallas kernels, exchange(): pl.pallas_call(kernel, out_shape=jax.ShapeDtypeStruct((2, bs, bs), full),...  79.8 us

profile of v5, /device:TPU:22, one launch (start us, length us, event | category | flops | bytes accessed | tf_op | source)
XLA Modules:
  0.0 83.5 jit_solution(10325746865955017621)
XLA Ops:
  0.0 0.0 copy-start.2
  0.0 0.1 compare_and_fusion
  0.1 1.4 %fusion.1.pairs = bf16[2,2,256,256]{3,2,1,0:T(8,128)(2,1)S(1)} fusion(f32[2,1,2,256,256]{4,3,2,1,0:T(8,128)} %param.6), kind=kLoop, calls=%fused_computation.3 | loop fusion | flops 262144 | bytes 1572864 | tf_op jit(solution)/shard_map/convert_element_type | solution.py:406
  1.4 0.1 copy-done.2
  1.5 0.0 copy-start
  1.5 0.0 copy-start.1
  1.5 0.1 fusion.known
  1.6 1.0 %copy-done = bf16[2,1,2,1,256,256]{5,4,3,2,1,0:T(8,128)(2,1)S(1)} copy-done((bf16[2,1,2,1,256,256]{5,4,3,2,1,0:T(8,128)(2,1)S(1)}, bf16[2,1,2,1,256,256]{5,4,3,2,1,0:T(8,128)(2,1)}, u32[]{:S(2)}) %copy-start) | copy-done | bytes 524312
  2.6 0.0 copy-done.1
  2.6 79.8 %shard_map.46 = f32[2,256,256]{2,1,0:T(8,128)S(1)} custom-call(bf16[2,2,256,256]{3,2,1,0:T(8,128)(2,1)S(1)} %bitcast.13, bf16[2,2,256,256]{3,2,1,0:T(8,128)(2,1)S(1)} %fusion.known, bf16[2,2,256,256]{3,2,1,0:T(8,128)(2,1)S(1)} %fusion.1.pairs, f32[32,256]{1,0:T(8,128)S(1)} %copy-done.1), custom_call_target="tpu_custom_call" | custom-call | tf_op jit(solution)/shard_map/pallas_call | solution.py:373
  82.4 1.1 %broadcast_select_fusion = f32[2,1,2,1,256,256]{5,4,3,2,1,0:T(8,128)} fusion(f32[2,1,2,1,256,256]{5,4,3,2,1,0:T(8,128)S(1)} %copy-done.2, f32[2,256,256]{2,1,0:T(8,128)S(1)} %shard_map.46, pred[2,2]{1,0:T(4,128)(4,1)S(1)} %compare_and_fusion), kind=kLoop, calls=%fused_computation.4 | loop fusion | flops 262144 | bytes 2621444 | tf_op jit(solution)/shard_map/jit(_where)/select_n | solution.py:413
  (1 shorter events, 0.0 us)
Async XLA Ops:
  0.0 1.5 %copy-start.2 = (f32[2,1,2,1,256,256]{5,4,3,2,1,0:T(8,128)S(1)}, f32[2,1,2,1,256,256]{5,4,3,2,1,0:T(8,128)}, u32[]{:S(2)}) copy-start(f32[2,1,2,1,256,256]{5,4,3,2,1,0:T(8,128)} %param.5) | copy-start | bytes 3145732
  1.5 1.0 %copy-start = (bf16[2,1,2,1,256,256]{5,4,3,2,1,0:T(8,128)(2,1)S(1)}, bf16[2,1,2,1,256,256]{5,4,3,2,1,0:T(8,128)(2,1)}, u32[]{:S(2)}) copy-start(bf16[2,1,2,1,256,256]{5,4,3,2,1,0:T(8,128)(2,1)} %param.4) | copy-start | bytes 1572868
  1.5 1.0 %copy-start.1 = (f32[32,256]{1,0:T(8,128)S(1)}, f32[32,256]{1,0:T(8,128)}, u32[]{:S(2)}) copy-start(f32[32,256]{1,0:T(8,128)} %lam.1) | copy-start | bytes 98308

commit v6 on v5

--- a/solution.py
+++ b/solution.py
@@ -13,9 +13,9 @@
 AWAY = 4
 MESH = pl.DeviceIdType.MESH
 
-SENDS = ("cF0", "cS0", "cF1", "cS1", "rF0", "rS0", "rF1", "rS1", "own", "x", "v")
-WAITS = (("0", "e", "1", "l", "2", "v0", "v1", "v2"), ("0", "e", "1", "l", "2", "3"))
-ENTRY = ((3, 3, 3, 3, 0, 0, 0, 0), (0, 0, 0, 0, 0, 1, 2, 3))
+SENDS = ("x", "cS0", "rS1", "rF0", "cF1", "rS0", "v", "own", "cF0", "cS1", "rF1")
+WAITS = (("e", "v0", "v1", "v2", "l", "2", "1", "0", "3"), ("0", "e", "1", "2", "3", "l"))
+ENTRY = ((3, 0, 0, 0, 0, 0, 0, 0), (0, 0, 0, 1, 0, 1, 2, 3))
 TURN = ((1, 1), (1, 1))
 CHAIN_ORDER = (4, 0, 5, 1, 6, 2, 7, 3)
 
@@ -59,9 +59,9 @@
 
 
 def kernel(
-    schur, known, pairs, lam, out,
-    ring, chain, near_s, vj, new_r, new_c, other, total, gap, fresh, solved,
-    q_ring, q_chain, q_near, q_vj, q_new_r, q_new_c, q_other, q_out,
+    schur, known_full, pairs_full, lam, out,
+    known, pairs, known_in, pairs_in, ring, chain, near_s, vj, new_r, new_c, other, total, gap, fresh, solved,
+    q_in, q_ring, q_chain, q_near, q_vj, q_new_r, q_new_c, q_other, q_out,
     s_src, s_ring, s_chain, s_v, s_own, s_near, s_new, s_out,
 ):
     r = lax.axis_index("row")
@@ -92,6 +92,13 @@
     def seat(i, second, x=x_at):
         return wrap(i + AWAY * second), XS * line_of(i, second) + x
 
+    fetch = [pltpu.make_async_copy(pairs_full, pairs_in, q_in.at[2])]
+    for t in (0, 1):
+        b = jnp.minimum((r + SIDE * t + e) // SIDE, 1)
+        fetch.append(pltpu.make_async_copy(known_full.at[t, b], known_in.at[t], q_in.at[t]))
+    for copy in fetch:
+        copy.start()
+
     barrier = pltpu.get_barrier_semaphore()
 
     def meet(row, col):
@@ -112,6 +119,10 @@
     others = XS * (XS - 1)
     lax.fori_loop(1, lines + 1, greet_line, 0)
     lax.fori_loop(0, others, greet_row, 0)
+    for copy in fetch:
+        copy.wait()
+    known[...] = known_in[...].astype(jnp.bfloat16)
+    pairs[...] = pairs_in[...].astype(jnp.bfloat16)
     pl.semaphore_wait(barrier, lines + 3 * others)
 
     near = e < FIRST
@@ -137,7 +148,7 @@
     def send_near(group, kind, t):
         k, j, b, to_ring, to_chain, entries, _ = places[t]
         n = "FS".index(kind)
-        src = (known, schur)[n].at[t, b]
+        src = (known.at[t], schur.at[t, b])[n]
         used = e >= n
         at = 2 * n + (group == "c")
         if group == "r":
@@ -373,9 +384,13 @@
     return pl.pallas_call(
         kernel,
         out_shape=jax.ShapeDtypeStruct((2, bs, bs), full),
-        in_specs=[vmem] * 4,
+        in_specs=[pl.BlockSpec(memory_space=pl.ANY)] * 3 + [vmem],
         out_specs=vmem,
         scratch_shapes=[
+            pltpu.VMEM((2, bs, bs), half),
+            pltpu.VMEM((2, 2, bs, bs), half),
+            pltpu.VMEM((2, bs, bs), full),
+            pltpu.VMEM((2, 2, bs, bs), full),
             pltpu.VMEM((band, bs, bs), half),
             pltpu.VMEM((band, bs, bs), half),
             pltpu.VMEM((DIAGS - 1, bs, bs), half),
@@ -387,13 +402,13 @@
             pltpu.VMEM((bs, bs), full),
             pltpu.VMEM((bs, bs), half),
             pltpu.VMEM((bs, bs), full),
-            dma((band,)), dma((band,)), dma((DIAGS - 1,)), dma((1,)),
+            dma((3,)), dma((band,)), dma((band,)), dma((DIAGS - 1,)), dma((1,)),
             dma((DIAGS - 1,)), dma((DIAGS - 1,)), dma((1,)), dma((2,)),
             dma((2, 5)), dma((band, 2)), dma((band, 2)), dma((1,)), dma((2, 2, DIAGS)),
             dma((2, DIAGS - 1)), dma((2, DIAGS - 1)), dma((2,)),
         ],
         compiler_params=pltpu.CompilerParams(
-            collective_id=0, has_side_effects=True, vmem_limit_bytes=40 * 1024 * 1024
+            collective_id=0, has_side_effects=True, vmem_limit_bytes=60 * 1024 * 1024
         ),
     )(schur, known, pairs, lam)
 
@@ -402,8 +417,8 @@
     known = known_blocks[:, 0, :, 0]
     solved = exchange(
         schur_blocks[:, 0, :, 0],
-        known.astype(jnp.bfloat16),
-        eigen_pairs[:, 0].astype(jnp.bfloat16),
+        known,
+        eigen_pairs[:, 0],
         eigenvalues,
     )
     rows = lax.axis_index("row") + SIDE * jnp.arange(2)[:, None]

time: 83.7 us -> 80 us (0.956)
  the two profiles are of different devices: /device:TPU:22 before, /device:TPU:25 now
where the time goes in v6:
time: 80 us; the launch traced here: 79.9 us
  Pallas kernels  77.6 us (97%)
  other arithmetic  2.27 us (3%)
    pallas_call x1, Pallas kernels, exchange(): pl.pallas_call(kernel, out_shape=jax.ShapeDtypeStruct((2, bs, bs), full),...  77.6 us
    select_n x1, other arithmetic, body(): output = jnp.where(new[:, :, None, None], solved[:, None], known)  2.18 us

profile of v6, /device:TPU:25, one launch (start us, length us, event | category | flops | bytes accessed | tf_op | source)
XLA Modules:
  0.0 79.9 jit_solution(13105459717666978576)
XLA Ops:
  0.0 0.1 compare_and_fusion
  0.1 0.0 copy-start
  0.1 77.6 %shard_map.46 = f32[2,256,256]{2,1,0:T(8,128)} custom-call(bf16[2,2,256,256]{3,2,1,0:T(8,128)(2,1)} %bitcast.5, f32[2,2,256,256]{3,2,1,0:T(8,128)} %bitcast.3, f32[2,2,256,256]{3,2,1,0:T(8,128)} %bitcast.4, f32[32,256]{1,0:T(8,128)} %lam.1), custom_call_target="tpu_custom_call" | custom-call | tf_op jit(solution)/shard_map/pallas_call | solution.py:384
  77.7 0.0 copy-done
  77.7 2.2 %broadcast_select_fusion = f32[2,1,2,1,256,256]{5,4,3,2,1,0:T(8,128)} fusion(f32[2,1,2,1,256,256]{5,4,3,2,1,0:T(8,128)S(1)} %copy-done, f32[2,256,256]{2,1,0:T(8,128)} %shard_map.46, pred[2,2]{1,0:T(4,128)(4,1)S(1)} %compare_and_fusion), kind=kLoop, calls=%fused_computation | loop fusion | flops 262144 | bytes 2621444 | tf_op jit(solution)/shard_map/jit(_where)/select_n | solution.py:428
  (1 shorter events, 0.0 us)
Async XLA Ops:
  0.1 77.6 %copy-start = (f32[2,1,2,1,256,256]{5,4,3,2,1,0:T(8,128)S(1)}, f32[2,1,2,1,256,256]{5,4,3,2,1,0:T(8,128)}, u32[]{:S(2)}) copy-start(f32[2,1,2,1,256,256]{5,4,3,2,1,0:T(8,128)} %param.5) | copy-start | bytes 3145732

commit v7 on v6

--- a/solution.py
+++ b/solution.py
@@ -13,11 +13,11 @@
 AWAY = 4
 MESH = pl.DeviceIdType.MESH
 
-SENDS = ("x", "cS0", "rS1", "rF0", "cF1", "rS0", "v", "own", "cF0", "cS1", "rF1")
-WAITS = (("e", "v0", "v1", "v2", "l", "2", "1", "0", "3"), ("0", "e", "1", "2", "3", "l"))
-ENTRY = ((3, 0, 0, 0, 0, 0, 0, 0), (0, 0, 0, 1, 0, 1, 2, 3))
-TURN = ((1, 1), (1, 1))
-CHAIN_ORDER = (4, 0, 5, 1, 6, 2, 7, 3)
+SENDS = ("cF0", "rF1", "rS0", "cF1", "rS1", "rF0", "cS0", "cS1", "v", "x", "own")
+WAITS = (("e", "3", "v0", "0", "1", "v2", "v1", "2", "l", "o"), ("e", "3", "0", "1", "2", "o", "l"))
+ENTRY = ((2, 1, 0, 2, 0, 2, 0, 0), (0, 0, 1, 0, 0, 1, 2, 2))
+TURN = ((1, 1), (1, -1))
+CHAIN_ORDER = (4, 7, 0, 3, 6, 2, 5, 1)
 
 
 def arrived(ref, sem):
@@ -111,8 +111,6 @@
     def greet_row(step, carry):
         col = XS * lax.rem(step, XS) + lax.rem(x_at + 1 + step // XS, XS)
         meet(r, col)
-        meet(wrap(r + AWAY), col)
-        meet(wrap(r - AWAY), col)
         return carry
 
     lines = SIDE * XS - 1
@@ -123,7 +121,7 @@
         copy.wait()
     known[...] = known_in[...].astype(jnp.bfloat16)
     pairs[...] = pairs_in[...].astype(jnp.bfloat16)
-    pl.semaphore_wait(barrier, lines + 3 * others)
+    pl.semaphore_wait(barrier, lines + others)
 
     near = e < FIRST
     eb = jnp.minimum(e, FIRST - 1)
@@ -159,11 +157,8 @@
     def send_own(t):
         k, j, b = places[t][:3]
         slot = FIRST + mo
-        for d in range(DIAGS):
-            fits = owner & (j + d < TOTAL) & (mo + d < DIAGS)
-            send(fits, schur.at[t, b], ring.at[slot], s_own.at[t, 0, d], q_ring.at[slot], *seat(k, 1, lax.rem(x_at + d, XS)))
-            fits = owned[t] & (mo + d < DIAGS) & (k >= d)
-            send_any(fits, schur.at[t, b], chain.at[slot], s_own.at[t, 1, d], q_chain.at[slot], *seat(jnp.maximum(k - d, 0), 0))
+        send(owned[t], schur.at[t, b], ring.at[slot], s_own.at[t, 0, 0], q_ring.at[slot], *seat(k, 1))
+        send_any(owned[t], schur.at[t, b], chain.at[slot], s_own.at[t, 1, 0], q_chain.at[slot], *seat(k, 0))
 
     def send_close(t):
         k, j, b = places[t][:3]
@@ -272,12 +267,25 @@
             arrived(vj, q_vj.at[0])
             v_copy().start()
 
+    def own_hop(n):
+        slot = FIRST + jnp.clip(m, 0, DIAGS - 1)
+        ref, sems = ((chain, q_chain), (ring, q_ring))[n]
+        run_if(adds[n], lambda: arrived(ref.at[slot], sems.at[slot]))
+        for d in range(1, DIAGS):
+            if n:
+                fits, to = j + d < TOTAL, (r, XS * y_at + lax.rem(x_at + d, XS))
+            else:
+                fits, to = i >= d, seat(jnp.maximum(i - d, 0), 0)
+            send(adds[n] & (m + d < DIAGS) & fits, ref.at[slot], ref.at[slot], s_own.at[2, n, d], sems.at[slot], *to)
+
     for n in (0, 1):
         for token in WAITS[n]:
             if token == "e":
                 ring_first(n, True)
             elif token == "l":
                 ring_second(n, True)
+            elif token == "o":
+                own_hop(n)
             elif token[0] == "v":
                 v_hop(int(token[1]))
             else:
@@ -304,8 +312,9 @@
     def far(x, carry):
         @pl.when(real & (x <= FIRST + m))
         def _():
-            run_if(~is_second, lambda: arrived(chain.at[x], q_chain.at[x]))
-            run_if(is_second, lambda: arrived(ring.at[x], q_ring.at[x]))
+            sent_on = x == FIRST + m
+            run_if(~is_second & ~sent_on, lambda: arrived(chain.at[x], q_chain.at[x]))
+            run_if(is_second & ~sent_on, lambda: arrived(ring.at[x], q_ring.at[x]))
             accumulate(x)
 
         return carry
@@ -404,7 +413,7 @@
             pltpu.VMEM((bs, bs), full),
             dma((3,)), dma((band,)), dma((band,)), dma((DIAGS - 1,)), dma((1,)),
             dma((DIAGS - 1,)), dma((DIAGS - 1,)), dma((1,)), dma((2,)),
-            dma((2, 5)), dma((band, 2)), dma((band, 2)), dma((1,)), dma((2, 2, DIAGS)),
+            dma((2, 5)), dma((band, 2)), dma((band, 2)), dma((1,)), dma((3, 2, DIAGS)),
             dma((2, DIAGS - 1)), dma((2, DIAGS - 1)), dma((2,)),
         ],
         compiler_params=pltpu.CompilerParams(

time: 80 us -> 75.5 us (0.944)
  the two profiles are of different devices: /device:TPU:25 before, /device:TPU:94 now
where the time goes in v7:
time: 75.5 us; the launch traced here: 75.4 us
  Pallas kernels  73.1 us (97%)
  other arithmetic  2.27 us (3%)
    pallas_call x1, Pallas kernels, exchange(): pl.pallas_call(kernel, out_shape=jax.ShapeDtypeStruct((2, bs, bs), full),...  73.1 us
    select_n x1, other arithmetic, body(): output = jnp.where(new[:, :, None, None], solved[:, None], known)  2.18 us

profile of v7, /device:TPU:94, one launch (start us, length us, event | category | flops | bytes accessed | tf_op | source)
XLA Modules:
  0.0 75.4 jit_solution(11587320771310054405)
XLA Ops:
  0.0 0.1 compare_and_fusion
  0.1 0.0 copy-start
  0.1 73.1 %shard_map.46 = f32[2,256,256]{2,1,0:T(8,128)} custom-call(bf16[2,2,256,256]{3,2,1,0:T(8,128)(2,1)} %bitcast.5, f32[2,2,256,256]{3,2,1,0:T(8,128)} %bitcast.3, f32[2,2,256,256]{3,2,1,0:T(8,128)} %bitcast.4, f32[32,256]{1,0:T(8,128)} %lam.1), custom_call_target="tpu_custom_call" | custom-call | tf_op jit(solution)/shard_map/pallas_call | solution.py:393
  73.2 0.0 copy-done
  73.2 2.2 %broadcast_select_fusion = f32[2,1,2,1,256,256]{5,4,3,2,1,0:T(8,128)} fusion(f32[2,1,2,1,256,256]{5,4,3,2,1,0:T(8,128)S(1)} %copy-done, f32[2,256,256]{2,1,0:T(8,128)} %shard_map.46, pred[2,2]{1,0:T(4,128)(4,1)S(1)} %compare_and_fusion), kind=kLoop, calls=%fused_computation | loop fusion | flops 262144 | bytes 2621444 | tf_op jit(solution)/shard_map/jit(_where)/select_n | solution.py:437
  (1 shorter events, 0.0 us)
Async XLA Ops:
  0.1 73.1 %copy-start = (f32[2,1,2,1,256,256]{5,4,3,2,1,0:T(8,128)S(1)}, f32[2,1,2,1,256,256]{5,4,3,2,1,0:T(8,128)}, u32[]{:S(2)}) copy-start(f32[2,1,2,1,256,256]{5,4,3,2,1,0:T(8,128)} %param.5) | copy-start | bytes 3145732

commit v8 on v7

--- a/solution.py
+++ b/solution.py
@@ -11,13 +11,14 @@
 XS = 4
 TOTAL = 32
 AWAY = 4
+LATE = 24
 MESH = pl.DeviceIdType.MESH
 
-SENDS = ("cF0", "rF1", "rS0", "cF1", "rS1", "rF0", "cS0", "cS1", "v", "x", "own")
-WAITS = (("e", "3", "v0", "0", "1", "v2", "v1", "2", "l", "o"), ("e", "3", "0", "1", "2", "o", "l"))
-ENTRY = ((2, 1, 0, 2, 0, 2, 0, 0), (0, 0, 1, 0, 0, 1, 2, 2))
+SENDS = ("cF0", "rF1", "v", "rS0", "rS1", "rF0", "cS0", "x", "cF1", "own", "cS1")
+WAITS = (("e", "3", "v0", "0", "1", "v1", "2", "l", "o", "v2"), ("3", "e", "0", "1", "2", "o", "l"))
+ENTRY = (((2, 1, 0, 2, 0, 1, 2, 1), (0, 1, 0, 2, 2, 2, 1, 1)), ((0, 0, 0, 2, 0, 1, 2, 2), (0, 1, 0, 0, 0, 1, 2, 2)))
 TURN = ((1, 1), (1, -1))
-CHAIN_ORDER = (4, 7, 0, 3, 6, 2, 5, 1)
+CHAIN_ORDER = (6, 5, 0, 7, 3, 2, 1, 4)
 
 
 def arrived(ref, sem):
@@ -33,10 +34,17 @@
 
 
 def pick(index, table):
+    if isinstance(index, int):
+        return table[index]
     chosen = jnp.int32(table[0])
     for n, value in enumerate(table[1:], 1):
         chosen = jnp.where(index == n, value, chosen)
     return chosen
+
+
+def entry_of(n, j, index):
+    early, late = ENTRY[n]
+    return jnp.where(j < LATE, pick(index, early), pick(index, late))
 
 
 def dot(a, b):
@@ -134,7 +142,7 @@
         to_ring = near & (k < TOTAL - FIRST)
         to_chain = near & (j >= FIRST) & (j < TOTAL)
         entries = [
-            seat(jnp.maximum(j - FIRST - jnp.minimum(pick(eb, ENTRY[n]), last), 0), n) for n in (0, 1)
+            seat(jnp.maximum(j - FIRST - jnp.minimum(entry_of(n, j, eb), last), 0), n) for n in (0, 1)
         ]
         v_entry = seat(jnp.maximum(j - FIRST - last, 0), 0)
         places.append((k, j, b, to_ring, to_chain, entries, v_entry))
@@ -243,7 +251,7 @@
                     copy.wait_send()
 
     def chain_moves(n, x):
-        at = jnp.minimum(ENTRY[n][x], last)
+        at = jnp.minimum(entry_of(n, j, x), last)
         up = adds[n] & (m >= at) & (m < last)
         down = adds[n] & (m <= at) & (m > 0)
         return up, down, jnp.abs(m - at)
@@ -353,6 +361,14 @@
             arrived(new_c.at[before], q_new_c.at[before])
             total[...] += dot(new_r[before], chain[away]) - dot(near_s[away - 1], new_c[before])
 
+    mine = jnp.minimum(m, DIAGS - 2)
+    onward = []
+    for d in range(1, DIAGS):
+        fits = adds[0] & (m + d < DIAGS)
+        in_ring = remote(fresh, new_r.at[mine], s_new.at[0, d - 1], q_new_r.at[mine], r, XS * y_at + lax.rem(x_at + d, XS))
+        in_chain = remote(fresh, new_c.at[mine], s_new.at[1, d - 1], q_new_c.at[mine], *seat(jnp.maximum(i - d, 0), 0))
+        onward += [(fits & (j + d < TOTAL), in_ring), (fits & (i >= d), in_chain)]
+
     @pl.when(adds[0])
     def _():
         x = left_dot(pairs[t, 1], total[...])
@@ -360,13 +376,11 @@
         x = left_dot(pairs[t, 0], x)
         x = right_dot(x, vj[1])
         fresh[...] = x.astype(jnp.bfloat16)
+        for fits, copy in onward:
+            run_if(fits, copy.start)
         solved[...] = x
 
-    mine = jnp.minimum(m, DIAGS - 2)
-    for d in range(1, DIAGS):
-        fits = adds[0] & (m + d < DIAGS)
-        send(fits & (j + d < TOTAL), fresh, new_r.at[mine], s_new.at[0, d - 1], q_new_r.at[mine], r, XS * y_at + lax.rem(x_at + d, XS))
-        send(fits & (i >= d), fresh, new_c.at[mine], s_new.at[1, d - 1], q_new_c.at[mine], *seat(jnp.maximum(i - d, 0), 0))
+    later.extend(onward)
     send_any(adds[0], solved, out.at[t], s_out.at[0], q_out.at[t], wrap(i), lax.rem(j, SIDE))
 
     for n in (0, 1):
@@ -393,7 +407,7 @@
     return pl.pallas_call(
         kernel,
         out_shape=jax.ShapeDtypeStruct((2, bs, bs), full),
-        in_specs=[pl.BlockSpec(memory_space=pl.ANY)] * 3 + [vmem],
+        in_specs=[pl.BlockSpec(memory_space=pltpu.HBM)] * 3 + [vmem],
         out_specs=vmem,
         scratch_shapes=[
             pltpu.VMEM((2, bs, bs), half),
@@ -417,9 +431,9 @@
             dma((2, DIAGS - 1)), dma((2, DIAGS - 1)), dma((2,)),
         ],
         compiler_params=pltpu.CompilerParams(
-            collective_id=0, has_side_effects=True, vmem_limit_bytes=60 * 1024 * 1024
+            collective_id=0, has_side_effects=True, vmem_limit_bytes=40 * 1024 * 1024
         ),
-    )(schur, known, pairs, lam)
+    )(*(pltpu.with_memory_space_constraint(a, pltpu.HBM) for a in (schur, known, pairs)), lam)
 
 
 def body(schur_blocks, known_blocks, eigen_pairs, eigenvalues):

time: 75.5 us -> 73.9 us (0.979)
  Pallas kernels: 73.1 us -> 71.8 us
  other arithmetic: 2.27 us -> 1.22 us
    pallas_call x1, Pallas kernels: 73.1 us -> 71.8 us  [exchange(): pl.pallas_call(kernel, out_shape=jax.ShapeDtypeStruct((2, bs, bs), full),...]
    select_n x1, other arithmetic: 2.18 us -> 1.14 us  [body(): output = jnp.where(new[:, :, None, None], solved[:, None], known)]
    unnamed x2 -> x4, local copies, waits for them, and re-layouts: 0.01 us -> 0.76 us
where the time goes in v8:
time: 73.9 us; the launch traced here: 73.8 us
  Pallas kernels  71.8 us (97%)
  other arithmetic  1.22 us (2%)
  local copies, waits for them, and re-layouts  0.76 us (1%)
    pallas_call x1, Pallas kernels, exchange(): pl.pallas_call(kernel, out_shape=jax.ShapeDtypeStruct((2, bs, bs), full),...  71.8 us

profile of v8, /device:TPU:94, one launch (start us, length us, event | category | flops | bytes accessed | tf_op | source)
XLA Modules:
  0.0 73.8 jit_solution(4800916802452129176)
XLA Ops:
  0.0 0.1 compare_and_fusion
  0.1 0.0 copy-start
  0.1 0.8 %copy-done = f32[32,256]{1,0:T(8,128)S(1)} copy-done((f32[32,256]{1,0:T(8,128)S(1)}, f32[32,256]{1,0:T(8,128)}, u32[]{:S(2)}) %copy-start) | copy-done | bytes 32792
  0.8 0.0 copy-start.1
  0.8 71.8 %shard_map.46 = f32[2,256,256]{2,1,0:T(8,128)S(1)} custom-call(bf16[2,2,256,256]{3,2,1,0:T(8,128)(2,1)} %bitcast.5, f32[2,2,256,256]{3,2,1,0:T(8,128)} %bitcast.3, f32[2,2,256,256]{3,2,1,0:T(8,128)} %bitcast.4, f32[32,256]{1,0:T(8,128)S(1)} %copy-done), custom_call_target="tpu_custom_call" | custom-call | tf_op jit(solution)/shard_map/pallas_call | solution.py:407
  72.6 0.0 copy-done.1
  72.6 1.1 %broadcast_select_fusion = f32[2,1,2,1,256,256]{5,4,3,2,1,0:T(8,128)} fusion(f32[2,1,2,1,256,256]{5,4,3,2,1,0:T(8,128)S(1)} %copy-done.1, f32[2,256,256]{2,1,0:T(8,128)S(1)} %shard_map.46, pred[2,2]{1,0:T(4,128)(4,1)S(1)} %compare_and_fusion), kind=kLoop, calls=%fused_computation | loop fusion | flops 262144 | bytes 2621444 | tf_op jit(solution)/shard_map/jit(_where)/select_n | solution.py:451
  (1 shorter events, 0.0 us)
Async XLA Ops:
  0.1 0.8 %copy-start = (f32[32,256]{1,0:T(8,128)S(1)}, f32[32,256]{1,0:T(8,128)}, u32[]{:S(2)}) copy-start(f32[32,256]{1,0:T(8,128)} %lam.1) | copy-start | bytes 98308
  0.8 71.8 %copy-start.1 = (f32[2,1,2,1,256,256]{5,4,3,2,1,0:T(8,128)S(1)}, f32[2,1,2,1,256,256]{5,4,3,2,1,0:T(8,128)}, u32[]{:S(2)}) copy-start(f32[2,1,2,1,256,256]{5,4,3,2,1,0:T(8,128)} %param.5) | copy-start | bytes 3145732

commit v9 on v8

--- a/solution.py
+++ b/solution.py
@@ -67,8 +67,8 @@
 
 
 def kernel(
-    schur, known_full, pairs_full, lam, out,
-    known, pairs, known_in, pairs_in, ring, chain, near_s, vj, new_r, new_c, other, total, gap, fresh, solved,
+    schur, known_full, pairs_full, lam_full, out,
+    lam, known, pairs, known_in, pairs_in, ring, chain, near_s, vj, new_r, new_c, other, total, gap, fresh, solved,
     q_in, q_ring, q_chain, q_near, q_vj, q_new_r, q_new_c, q_other, q_out,
     s_src, s_ring, s_chain, s_v, s_own, s_near, s_new, s_out,
 ):
@@ -100,7 +100,10 @@
     def seat(i, second, x=x_at):
         return wrap(i + AWAY * second), XS * line_of(i, second) + x
 
-    fetch = [pltpu.make_async_copy(pairs_full, pairs_in, q_in.at[2])]
+    fetch = [
+        pltpu.make_async_copy(pairs_full, pairs_in, q_in.at[2]),
+        pltpu.make_async_copy(lam_full, lam, q_in.at[3]),
+    ]
     for t in (0, 1):
         b = jnp.minimum((r + SIDE * t + e) // SIDE, 1)
         fetch.append(pltpu.make_async_copy(known_full.at[t, b], known_in.at[t], q_in.at[t]))
@@ -407,9 +410,10 @@
     return pl.pallas_call(
         kernel,
         out_shape=jax.ShapeDtypeStruct((2, bs, bs), full),
-        in_specs=[pl.BlockSpec(memory_space=pltpu.HBM)] * 3 + [vmem],
+        in_specs=[pl.BlockSpec(memory_space=pltpu.HBM)] * 4,
         out_specs=vmem,
         scratch_shapes=[
+            pltpu.VMEM(lam.shape, full),
             pltpu.VMEM((2, bs, bs), half),
             pltpu.VMEM((2, 2, bs, bs), half),
             pltpu.VMEM((2, bs, bs), full),
@@ -425,7 +429,7 @@
             pltpu.VMEM((bs, bs), full),
             pltpu.VMEM((bs, bs), half),
             pltpu.VMEM((bs, bs), full),
-            dma((3,)), dma((band,)), dma((band,)), dma((DIAGS - 1,)), dma((1,)),
+            dma((4,)), dma((band,)), dma((band,)), dma((DIAGS - 1,)), dma((1,)),
             dma((DIAGS - 1,)), dma((DIAGS - 1,)), dma((1,)), dma((2,)),
             dma((2, 5)), dma((band, 2)), dma((band, 2)), dma((1,)), dma((3, 2, DIAGS)),
             dma((2, DIAGS - 1)), dma((2, DIAGS - 1)), dma((2,)),
@@ -433,7 +437,7 @@
         compiler_params=pltpu.CompilerParams(
             collective_id=0, has_side_effects=True, vmem_limit_bytes=40 * 1024 * 1024
         ),
-    )(*(pltpu.with_memory_space_constraint(a, pltpu.HBM) for a in (schur, known, pairs)), lam)
+    )(*(pltpu.with_memory_space_constraint(a, pltpu.HBM) for a in (schur, known, pairs, lam)))
 
 
 def body(schur_blocks, known_blocks, eigen_pairs, eigenvalues):

time: 73.9 us -> 73.4 us (level)
  local copies, waits for them, and re-layouts: 0.76 us -> 0.01 us
    unnamed x4 -> x2, local copies, waits for them, and re-layouts: 0.76 us -> 0.01 us
where the time goes in v9:
time: 73.4 us; the launch traced here: 73.3 us
  Pallas kernels  72.1 us (98%)
  other arithmetic  1.22 us (2%)
    pallas_call x1, Pallas kernels, exchange(): pl.pallas_call(kernel, out_shape=jax.ShapeDtypeStruct((2, bs, bs), full),...  72.1 us

profile of v9, /device:TPU:94, one launch (start us, length us, event | category | flops | bytes accessed | tf_op | source)
XLA Modules:
  0.0 73.3 jit_solution(11852016990710380799)
XLA Ops:
  0.0 0.1 compare_and_fusion
  0.1 0.0 copy-start
  0.1 72.1 %shard_map.46 = f32[2,256,256]{2,1,0:T(8,128)S(1)} custom-call(bf16[2,2,256,256]{3,2,1,0:T(8,128)(2,1)} %bitcast.5, f32[2,2,256,256]{3,2,1,0:T(8,128)} %bitcast.3, f32[2,2,256,256]{3,2,1,0:T(8,128)} %bitcast.4, f32[32,256]{1,0:T(8,128)} %lam_full.1), custom_call_target="tpu_custom_call" | custom-call | tf_op jit(solution)/shard_map/pallas_call | solution.py:410
  72.2 0.0 copy-done
  72.2 1.1 %broadcast_select_fusion = f32[2,1,2,1,256,256]{5,4,3,2,1,0:T(8,128)} fusion(f32[2,1,2,1,256,256]{5,4,3,2,1,0:T(8,128)S(1)} %copy-done, f32[2,256,256]{2,1,0:T(8,128)S(1)} %shard_map.46, pred[2,2]{1,0:T(4,128)(4,1)S(1)} %compare_and_fusion), kind=kLoop, calls=%fused_computation | loop fusion | flops 262144 | bytes 2621444 | tf_op jit(solution)/shard_map/jit(_where)/select_n | solution.py:455
  (1 shorter events, 0.0 us)
Async XLA Ops:
  0.1 72.1 %copy-start = (f32[2,1,2,1,256,256]{5,4,3,2,1,0:T(8,128)S(1)}, f32[2,1,2,1,256,256]{5,4,3,2,1,0:T(8,128)}, u32[]{:S(2)}) copy-start(f32[2,1,2,1,256,256]{5,4,3,2,1,0:T(8,128)} %param.5) | copy-start | bytes 3145732

commit v10 on v9

--- a/solution.py
+++ b/solution.py
@@ -14,11 +14,11 @@
 LATE = 24
 MESH = pl.DeviceIdType.MESH
 
-SENDS = ("cF0", "rF1", "v", "rS0", "rS1", "rF0", "cS0", "x", "cF1", "own", "cS1")
-WAITS = (("e", "3", "v0", "0", "1", "v1", "2", "l", "o", "v2"), ("3", "e", "0", "1", "2", "o", "l"))
-ENTRY = (((2, 1, 0, 2, 0, 1, 2, 1), (0, 1, 0, 2, 2, 2, 1, 1)), ((0, 0, 0, 2, 0, 1, 2, 2), (0, 1, 0, 0, 0, 1, 2, 2)))
-TURN = ((1, 1), (1, -1))
-CHAIN_ORDER = (6, 5, 0, 7, 3, 2, 1, 4)
+SENDS = ("rS1", "rF1", "cF0", "rF0", "rS0", "cF1", "x", "own", "cS0", "v", "cS1")
+WAITS = (("e", "0", "v1", "v0", "1", "2", "3", "o", "l", "v2"), ("e", "0", "1", "2", "l", "o", "3"))
+ENTRY = (((3, 1, 1, 2, 0, 1, 1, 1), (0, 1, 0, 2, 1, 0, 1, 1)), ((1, 0, 0, 0, 0, 1, 2, 2), (0, 1, 0, 0, 0, 1, 2, 3)))
+TURN = ((1, -1), (1, -1))
+CHAIN_ORDER = (0, 5, 7, 3, 6, 1, 2, 4)
 
 
 def arrived(ref, sem):

time: 73.4 us -> 72.7 us (level)
  no operation moved by 1% of the time
where the time goes in v10:
time: 72.7 us; the launch traced here: 72.6 us
  Pallas kernels  71.4 us (98%)
  other arithmetic  1.22 us (2%)
    pallas_call x1, Pallas kernels, exchange(): pl.pallas_call(kernel, out_shape=jax.ShapeDtypeStruct((2, bs, bs), full),...  71.4 us

profile of v10, /device:TPU:94, one launch (start us, length us, event | category | flops | bytes accessed | tf_op | source)
XLA Modules:
  0.0 72.6 jit_solution(12905769242991906742)
XLA Ops:
  0.0 0.1 compare_and_fusion
  0.1 0.0 copy-start
  0.1 71.4 %shard_map.46 = f32[2,256,256]{2,1,0:T(8,128)S(1)} custom-call(bf16[2,2,256,256]{3,2,1,0:T(8,128)(2,1)} %bitcast.5, f32[2,2,256,256]{3,2,1,0:T(8,128)} %bitcast.3, f32[2,2,256,256]{3,2,1,0:T(8,128)} %bitcast.4, f32[32,256]{1,0:T(8,128)} %lam_full.1), custom_call_target="tpu_custom_call" | custom-call | tf_op jit(solution)/shard_map/pallas_call | solution.py:410
  71.5 0.0 copy-done
  71.5 1.1 %broadcast_select_fusion = f32[2,1,2,1,256,256]{5,4,3,2,1,0:T(8,128)} fusion(f32[2,1,2,1,256,256]{5,4,3,2,1,0:T(8,128)S(1)} %copy-done, f32[2,256,256]{2,1,0:T(8,128)S(1)} %shard_map.46, pred[2,2]{1,0:T(4,128)(4,1)S(1)} %compare_and_fusion), kind=kLoop, calls=%fused_computation | loop fusion | flops 262144 | bytes 2621444 | tf_op jit(solution)/shard_map/jit(_where)/select_n | solution.py:455
  (1 shorter events, 0.0 us)
Async XLA Ops:
  0.1 71.4 %copy-start = (f32[2,1,2,1,256,256]{5,4,3,2,1,0:T(8,128)S(1)}, f32[2,1,2,1,256,256]{5,4,3,2,1,0:T(8,128)}, u32[]{:S(2)}) copy-start(f32[2,1,2,1,256,256]{5,4,3,2,1,0:T(8,128)} %param.5) | copy-start | bytes 3145732

commit v11 on v10

--- a/solution.py
+++ b/solution.py
@@ -14,11 +14,11 @@
 LATE = 24
 MESH = pl.DeviceIdType.MESH
 
-SENDS = ("rS1", "rF1", "cF0", "rF0", "rS0", "cF1", "x", "own", "cS0", "v", "cS1")
-WAITS = (("e", "0", "v1", "v0", "1", "2", "3", "o", "l", "v2"), ("e", "0", "1", "2", "l", "o", "3"))
-ENTRY = (((3, 1, 1, 2, 0, 1, 1, 1), (0, 1, 0, 2, 1, 0, 1, 1)), ((1, 0, 0, 0, 0, 1, 2, 2), (0, 1, 0, 0, 0, 1, 2, 3)))
-TURN = ((1, -1), (1, -1))
-CHAIN_ORDER = (0, 5, 7, 3, 6, 1, 2, 4)
+SENDS = ("rS1", "cF0", "rF0", "rF1", "rS0", "x", "v", "cS1", "own", "cF1", "cS0")
+WAITS = (("0", "e", "v1", "v0", "1", "2", "o", "l", "3", "v2"), ("e", "0", "1", "2", "l", "3", "o"))
+ENTRY = (((0, 1, 1, 2, 0, 1, 1, 1), (0, 1, 0, 2, 1, 0, 1, 1)), ((1, 0, 0, 0, 0, 1, 2, 2), (0, 1, 0, 0, 0, 1, 1, 3)))
+TURN = ((-1, -1), (1, -1))
+CHAIN_ORDER = (5, 7, 3, 0, 6, 1, 2, 4)
 
 
 def arrived(ref, sem):

time: 72.7 us -> 72.4 us (level)
  no operation moved by 1% of the time
where the time goes in v11:
time: 72.4 us; the launch traced here: 72.3 us
  Pallas kernels  71 us (98%)
  other arithmetic  1.22 us (2%)
    pallas_call x1, Pallas kernels, exchange(): pl.pallas_call(kernel, out_shape=jax.ShapeDtypeStruct((2, bs, bs), full),...  71 us

profile of v11, /device:TPU:94, one launch (start us, length us, event | category | flops | bytes accessed | tf_op | source)
XLA Modules:
  0.0 72.3 jit_solution(3647025953401558341)
XLA Ops:
  0.0 0.1 compare_and_fusion
  0.1 0.0 copy-start
  0.1 71.0 %shard_map.46 = f32[2,256,256]{2,1,0:T(8,128)S(1)} custom-call(bf16[2,2,256,256]{3,2,1,0:T(8,128)(2,1)} %bitcast.5, f32[2,2,256,256]{3,2,1,0:T(8,128)} %bitcast.3, f32[2,2,256,256]{3,2,1,0:T(8,128)} %bitcast.4, f32[32,256]{1,0:T(8,128)} %lam_full.1), custom_call_target="tpu_custom_call" | custom-call | tf_op jit(solution)/shard_map/pallas_call | solution.py:410
  71.1 0.0 copy-done
  71.1 1.1 %broadcast_select_fusion = f32[2,1,2,1,256,256]{5,4,3,2,1,0:T(8,128)} fusion(f32[2,1,2,1,256,256]{5,4,3,2,1,0:T(8,128)S(1)} %copy-done, f32[2,256,256]{2,1,0:T(8,128)S(1)} %shard_map.46, pred[2,2]{1,0:T(4,128)(4,1)S(1)} %compare_and_fusion), kind=kLoop, calls=%fused_computation | loop fusion | flops 262144 | bytes 2621444 | tf_op jit(solution)/shard_map/jit(_where)/select_n | solution.py:455
  (1 shorter events, 0.0 us)
Async XLA Ops:
  0.1 71.1 %copy-start = (f32[2,1,2,1,256,256]{5,4,3,2,1,0:T(8,128)S(1)}, f32[2,1,2,1,256,256]{5,4,3,2,1,0:T(8,128)}, u32[]{:S(2)}) copy-start(f32[2,1,2,1,256,256]{5,4,3,2,1,0:T(8,128)} %param.5) | copy-start | bytes 3145732

commit v12 on v11

--- a/solution.py
+++ b/solution.py
@@ -14,11 +14,12 @@
 LATE = 24
 MESH = pl.DeviceIdType.MESH
 
-SENDS = ("rS1", "cF0", "rF0", "rF1", "rS0", "x", "v", "cS1", "own", "cF1", "cS0")
-WAITS = (("0", "e", "v1", "v0", "1", "2", "o", "l", "3", "v2"), ("e", "0", "1", "2", "l", "3", "o"))
-ENTRY = (((0, 1, 1, 2, 0, 1, 1, 1), (0, 1, 0, 2, 1, 0, 1, 1)), ((1, 0, 0, 0, 0, 1, 2, 2), (0, 1, 0, 0, 0, 1, 1, 3)))
+SENDS = ("rF1", "own", "rS0", "v", "cS0", "rF0", "rS1", "cF1", "x", "cF0", "cS1")
+WAITS = (("e", "0", "l", "3", "1", "v0", "v2", "v1", "o", "2"), ("0", "3", "e", "o", "1", "2", "l"))
+ENTRY = (((3, 3, 1, 0, 0, 1, 1, 1), (1, 1, 0, 0, 1, 1, 2, 1)), ((1, 0, 3, 0, 0, 0, 2, 2), (0, 1, 0, 2, 0, 1, 3, 3)))
 TURN = ((-1, -1), (1, -1))
-CHAIN_ORDER = (5, 7, 3, 0, 6, 1, 2, 4)
+SUMS = ((6, 2, 5, 4, 3, 7, 1), (1, 4, 7, 2, 6, 3, 5))
+CHAIN_ORDER = (6, 5, 7, 0, 3, 4, 2, 1)
 
 
 def arrived(ref, sem):
@@ -331,10 +332,10 @@
         return carry
 
     lax.fori_loop(FIRST, FIRST + DIAGS, far, 0)
-    for x in range(1, FIRST):
-        chain_rest(0, x)
-        ring_rest(1, x)
-        run_if(real & (x > m), lambda: accumulate(x))
+    for n in (0, 1):
+        for x in SUMS[n]:
+            ring_rest(1, x) if n else chain_rest(0, x)
+            run_if(adds[n] & (x > m), lambda: accumulate(x))
 
     @pl.when(adds[1])
     def _():

time: 72.4 us -> 72.4 us (level)
  the two profiles are of different devices: /device:TPU:94 before, /device:TPU:22 now
where the time goes in v12:
time: 72.4 us; the launch traced here: 72.3 us
  Pallas kernels  71.1 us (98%)
  other arithmetic  1.22 us (2%)
    pallas_call x1, Pallas kernels, exchange(): pl.pallas_call(kernel, out_shape=jax.ShapeDtypeStruct((2, bs, bs), full),...  71.1 us

profile of v12, /device:TPU:22, one launch (start us, length us, event | category | flops | bytes accessed | tf_op | source)
XLA Modules:
  0.0 72.3 jit_solution(7968282783936799537)
XLA Ops:
  0.0 0.1 compare_and_fusion
  0.1 0.0 copy-start
  0.1 71.1 %shard_map.46 = f32[2,256,256]{2,1,0:T(8,128)S(1)} custom-call(bf16[2,2,256,256]{3,2,1,0:T(8,128)(2,1)} %bitcast.5, f32[2,2,256,256]{3,2,1,0:T(8,128)} %bitcast.3, f32[2,2,256,256]{3,2,1,0:T(8,128)} %bitcast.4, f32[32,256]{1,0:T(8,128)} %lam_full.1), custom_call_target="tpu_custom_call" | custom-call | tf_op jit(solution)/shard_map/pallas_call | solution.py:411
  71.2 0.0 copy-done
  71.2 1.1 %broadcast_select_fusion = f32[2,1,2,1,256,256]{5,4,3,2,1,0:T(8,128)} fusion(f32[2,1,2,1,256,256]{5,4,3,2,1,0:T(8,128)S(1)} %copy-done, f32[2,256,256]{2,1,0:T(8,128)S(1)} %shard_map.46, pred[2,2]{1,0:T(4,128)(4,1)S(1)} %compare_and_fusion), kind=kLoop, calls=%fused_computation | loop fusion | flops 262144 | bytes 2621444 | tf_op jit(solution)/shard_map/jit(_where)/select_n | solution.py:456
  (1 shorter events, 0.0 us)
Async XLA Ops:
  0.1 71.1 %copy-start = (f32[2,1,2,1,256,256]{5,4,3,2,1,0:T(8,128)S(1)}, f32[2,1,2,1,256,256]{5,4,3,2,1,0:T(8,128)}, u32[]{:S(2)}) copy-start(f32[2,1,2,1,256,256]{5,4,3,2,1,0:T(8,128)} %param.5) | copy-start | bytes 3145732

commit v13 on v11

--- a/solution.py
+++ b/solution.py
@@ -16,7 +16,7 @@
 
 SENDS = ("rS1", "cF0", "rF0", "rF1", "rS0", "x", "v", "cS1", "own", "cF1", "cS0")
 WAITS = (("0", "e", "v1", "v0", "1", "2", "o", "l", "3", "v2"), ("e", "0", "1", "2", "l", "3", "o"))
-ENTRY = (((0, 1, 1, 2, 0, 1, 1, 1), (0, 1, 0, 2, 1, 0, 1, 1)), ((1, 0, 0, 0, 0, 1, 2, 2), (0, 1, 0, 0, 0, 1, 1, 3)))
+ENTRY = (((0, 1, 1, 2, 0, 1, 1, 1), (0, 0, 0, 2, 0, 0, 1, 1)), ((1, 0, 0, 0, 0, 1, 2, 2), (0, 1, 0, 0, 0, 1, 1, 3)))
 TURN = ((-1, -1), (1, -1))
 CHAIN_ORDER = (5, 7, 3, 0, 6, 1, 2, 4)
 

time: 72.4 us -> 72.4 us (level)
  no operation moved by 1% of the time
where the time goes in v13:
time: 72.4 us; the launch traced here: 72.3 us
  Pallas kernels  71 us (98%)
  other arithmetic  1.22 us (2%)
    pallas_call x1, Pallas kernels, exchange(): pl.pallas_call(kernel, out_shape=jax.ShapeDtypeStruct((2, bs, bs), full),...  71 us

profile of v13, /device:TPU:94, one launch (start us, length us, event | category | flops | bytes accessed | tf_op | source)
XLA Modules:
  0.0 72.3 jit_solution(1956614900247251899)
XLA Ops:
  0.0 0.1 compare_and_fusion
  0.1 0.0 copy-start
  0.1 71.0 %shard_map.46 = f32[2,256,256]{2,1,0:T(8,128)S(1)} custom-call(bf16[2,2,256,256]{3,2,1,0:T(8,128)(2,1)} %bitcast.5, f32[2,2,256,256]{3,2,1,0:T(8,128)} %bitcast.3, f32[2,2,256,256]{3,2,1,0:T(8,128)} %bitcast.4, f32[32,256]{1,0:T(8,128)} %lam_full.1), custom_call_target="tpu_custom_call" | custom-call | tf_op jit(solution)/shard_map/pallas_call | solution.py:410
  71.1 0.0 copy-done
  71.1 1.1 %broadcast_select_fusion = f32[2,1,2,1,256,256]{5,4,3,2,1,0:T(8,128)} fusion(f32[2,1,2,1,256,256]{5,4,3,2,1,0:T(8,128)S(1)} %copy-done, f32[2,256,256]{2,1,0:T(8,128)S(1)} %shard_map.46, pred[2,2]{1,0:T(4,128)(4,1)S(1)} %compare_and_fusion), kind=kLoop, calls=%fused_computation | loop fusion | flops 262144 | bytes 2621444 | tf_op jit(solution)/shard_map/jit(_where)/select_n | solution.py:455
  (1 shorter events, 0.0 us)
Async XLA Ops:
  0.1 71.1 %copy-start = (f32[2,1,2,1,256,256]{5,4,3,2,1,0:T(8,128)S(1)}, f32[2,1,2,1,256,256]{5,4,3,2,1,0:T(8,128)}, u32[]{:S(2)}) copy-start(f32[2,1,2,1,256,256]{5,4,3,2,1,0:T(8,128)} %param.5) | copy-start | bytes 3145732
